TPU v7x, 32 devices: a whole 2x2x4 slice. The times are simulated.
32 devices in a mesh: fsdp: 4 (over y, x), context: 4 (over z), tensor: 2 (over core).
Axes of the slice: x: 2, y: 2, z: 4, core: 2. Of those that a mesh axis runs over, the one named last changes fastest.
Arguments:
- inputs: bfloat16 [2048, 1024], P(('fsdp', 'context')), may hold values from -6 to 6
- seq_lengths: int32 [4, 2], P('fsdp'), may hold values from 170 to 342, as said below
- norm_gains: bfloat16 [2, 1024], P(None, ('fsdp', 'context')), may hold values from 0.5 to 1.5
- mamba_in: bfloat16 [1024, 2, 1536], P(('fsdp', 'context'), None, 'tensor'), may hold values from -0.1875 to 0.1875
- dt_proj: bfloat16 [1024, 24], P(('fsdp', 'context'), 'tensor'), may hold values from -0.1875 to 0.1875
- bc_proj: bfloat16 [1024, 256], P(('fsdp', 'context')), may hold values from -0.1875 to 0.1875
- mamba_chan: bfloat16 [24, 384], P('tensor', ('fsdp', 'context')), may hold values from -0.5 to 1.25
- bc_conv: bfloat16 [5, 256], P(None, ('fsdp', 'context')), may hold values from -0.5 to 0.5
- head_params: float32 [3, 24], P(None, 'tensor'), may hold values from -10 to 3, as said below
- query_proj: bfloat16 [1024, 512], P(('fsdp', 'context'), 'tensor'), may hold values from -0.1875 to 0.1875
- kv_proj: bfloat16 [1024, 2, 128], P(('fsdp', 'context'), None, 'tensor'), may hold values from -0.1875 to 0.1875
- attn_out: bfloat16 [512, 1024], P('tensor', ('fsdp', 'context')), may hold values from -3 to 3
- mamba_out: bfloat16 [1536, 1024], P('tensor', ('fsdp', 'context')), may hold values from -0.15625 to 0.15625
- mlp_in: bfloat16 [1024, 2, 2048], P(('fsdp', 'context'), None, 'tensor'), may hold values from -0.1875 to 0.1875
- mlp_out: bfloat16 [2048, 1024], P('tensor', ('fsdp', 'context')), may hold values from -0.125 to 0.125
- out_grad: bfloat16 [2048, 1024], P(('fsdp', 'context')), may hold values from -6 to 6
Outputs:
- output: bfloat16 [2048, 1024], P(('fsdp', 'context'))
- input_grad: float32 [2048, 1024], P(('fsdp', 'context'))
- grad_norm_gains: float32 [2, 1024], P(None, ('fsdp', 'context'))
- grad_mamba_in: float32 [1024, 2, 1536], P(('fsdp', 'context'), None, 'tensor')
- grad_dt_proj: float32 [1024, 24], P(('fsdp', 'context'), 'tensor')
- grad_bc_proj: float32 [1024, 256], P(('fsdp', 'context'))
- grad_mamba_chan: float32 [24, 384], P('tensor', ('fsdp', 'context'))
- grad_bc_conv: float32 [5, 256], P(None, ('fsdp', 'context'))
- grad_head_params: float32 [3, 24], P(None, 'tensor')
- grad_query_proj: float32 [1024, 512], P(('fsdp', 'context'), 'tensor')
- grad_kv_proj: float32 [1024, 2, 128], P(('fsdp', 'context'), None, 'tensor')
- grad_attn_out: float32 [512, 1024], P('tensor', ('fsdp', 'context'))
- grad_mamba_out: float32 [1536, 1024], P('tensor', ('fsdp', 'context'))
- grad_mlp_in: float32 [1024, 2, 2048], P(('fsdp', 'context'), None, 'tensor')
- grad_mlp_out: float32 [2048, 1024], P('tensor', ('fsdp', 'context'))
Inputs may be any that keep to these rules, and one draw needn't show every extreme that they name: `seq_lengths`: row g lists, in order, the lengths of the 2 sequences that fill the 512 rows of token group g; they sum to 512. `head_params`: rows are step bias, log decay rate and skip weight of a head.
All inputs are finite; a program needn't handle non-finite values.
Results may differ from a plain program's by a relative error of at most 0.018.
Values may be sent and summed in bfloat16 or wider, within the bound.
No kernel may reach another device: no remote copies, remote signals or barrier semaphores. Data moves between devices by JAX's collectives and lax.ppermute only.
A program may use at most 128 MiB of HBM per device.

v0:
```python
import jax
import jax.numpy as jnp
from jax import lax
from jax.sharding import PartitionSpec as P

MH = 24
HDIM = 64
NSTATE = 128
KCONV = 4


NORM_EPS = 1e-05
ROPE_BASE = 100000000000.0
PRECISE = lax.Precision.HIGHEST


def from_behind(block, axis, distance):
    devices = range(lax.axis_size(axis))
    route = [(i - distance, i) for i in devices if i - distance in devices]
    return lax.ppermute(block, axis, route)


def entering(shard, axis, join, neutral):
    place = lax.axis_index(axis)
    gathered = jax.tree.map(
        lambda a, kind: lax.all_gather(a.astype(kind), axis), shard, (jnp.bfloat16, jnp.bfloat16)
    )
    state = jax.tree.map(lambda a, e: jnp.zeros_like(a) + jnp.asarray(e, a.dtype), shard, neutral)

    def one(turn, state):
        return join(
            state,
            jax.tree.map(
                lambda a, own: lax.dynamic_index_in_dim(a, turn, 0, False).astype(own.dtype),
                gathered,
                shard,
            ),
        )

    return lax.fori_loop(0, place, one, state)


def entering_2(shard, axis, join, neutral):
    count = lax.axis_size(axis)
    place = lax.axis_index(axis)
    ahead = count - 1 - place
    gathered = jax.tree.map(
        lambda a, kind: lax.all_gather(a.astype(kind), axis),
        shard,
        jax.tree.map(lambda a: jnp.bfloat16 if a.dtype == jnp.float32 else a.dtype, shard),
    )
    state = jax.tree.map(lambda a, e: jnp.zeros_like(a) + jnp.asarray(e, a.dtype), shard, neutral)

    def one(turn, state):
        source = count - 1 - turn
        return join(
            state,
            jax.tree.map(
                lambda a, own: lax.dynamic_index_in_dim(a, source, 0, False).astype(own.dtype),
                gathered,
                shard,
            ),
        )

    return lax.fori_loop(0, ahead, one, state)


def silu_grad(values):
    sigma = jax.nn.sigmoid(values)
    return sigma * (1.0 + values * (1.0 - sigma))


def rms_forward(values):
    inv_rms = lax.rsqrt(jnp.mean(values * values, axis=-1, keepdims=True) + NORM_EPS)
    return (values * inv_rms, inv_rms)


def rms_backward(grad_out, normed, inv_rms, gain_vec):
    grad_normed = grad_out * gain_vec[None, :]
    grad_values = inv_rms * (
        grad_normed - normed * jnp.mean(grad_normed * normed, axis=-1, keepdims=True)
    )
    return (grad_values, jnp.sum(grad_out * normed, axis=0))


def rope_tables(positions, head_width):
    half_width = head_width // 2
    freqs = jnp.power(ROPE_BASE, -jnp.arange(half_width).astype(jnp.float32) * (2.0 / head_width))
    angles = positions.astype(jnp.float32)[:, None] * freqs[None, :]
    angles = jnp.concatenate([angles, angles], axis=1)
    return (jnp.cos(angles), jnp.sin(angles))


def rotate_half(values):
    half_width = values.shape[-1] // 2
    return jnp.concatenate([-values[..., half_width:], values[..., :half_width]], axis=-1)


def apply_rope(values, cosine, sine):
    return values * cosine[:, None, :] + rotate_half(values) * sine[:, None, :]


def undo_rope(grads, cosine, sine):
    return grads * cosine[:, None, :] - rotate_half(grads) * sine[:, None, :]


def sequence_layout(lengths_row, row_start, row_count):
    starts = jnp.cumsum(lengths_row) - lengths_row
    row_ids = row_start + jnp.arange(row_count, dtype=jnp.int32)
    inside = row_ids[:, None] >= starts[None, :]
    seq_ids = jnp.sum(inside.astype(jnp.int32), axis=1) - 1
    seq_start = jnp.max(jnp.where(inside, starts[None, :], 0), axis=1)
    return (seq_ids, row_ids - seq_start)


def conv_block(extended, conv_taps, conv_bias, ids_ext):
    num_taps = conv_taps.shape[0]
    row_count = extended.shape[0] - num_taps + 1
    current = ids_ext[num_taps - 1 :]
    total = jnp.zeros((row_count, extended.shape[1]), jnp.float32) + conv_bias[None, :]
    for offset in range(num_taps):
        same_seq = (ids_ext[offset : offset + row_count] == current).astype(jnp.float32)
        total = (
            total
            + conv_taps[offset][None, :] * extended[offset : offset + row_count] * same_seq[:, None]
        )
    return total


def unpack_chan(chan_all, conv_all):
    num_heads = chan_all.shape[0]
    head_width = chan_all.shape[1] // (KCONV + 2)
    chan_wide = chan_all.astype(jnp.float32)
    conv_wide = conv_all.astype(jnp.float32)
    taps_x = jnp.transpose(
        chan_wide[:, : KCONV * head_width].reshape(num_heads, KCONV, head_width), (1, 0, 2)
    ).reshape(KCONV, num_heads * head_width)
    bias_x = chan_wide[:, KCONV * head_width : (KCONV + 1) * head_width].reshape(-1)
    norm_gain = chan_wide[:, (KCONV + 1) * head_width :].reshape(-1)
    return (
        jnp.concatenate([taps_x, conv_wide[:KCONV]], axis=1),
        jnp.concatenate([bias_x, conv_wide[KCONV]]),
        norm_gain,
    )


def pack_chan_grads(grad_taps, grad_bias, grad_gain, num_heads):
    chan_x = grad_gain.shape[0]
    head_width = chan_x // num_heads
    taps_x = jnp.transpose(
        grad_taps[:, :chan_x].reshape(KCONV, num_heads, head_width), (1, 0, 2)
    ).reshape(num_heads, KCONV * head_width)
    chan_grad = jnp.concatenate(
        [
            taps_x,
            grad_bias[:chan_x].reshape(num_heads, head_width),
            grad_gain.reshape(num_heads, head_width),
        ],
        axis=1,
    )
    conv_grad = jnp.concatenate([grad_taps[:, chan_x:], grad_bias[chan_x:][None, :]], axis=0)
    return (chan_grad, conv_grad)


def head_rates(dt_raw, head_vec):
    dt_step = jax.nn.softplus(dt_raw + head_vec[0][None, :])
    log_cum = jnp.cumsum(-dt_step * jnp.exp(head_vec[1])[None, :], axis=0)
    return (dt_step, log_cum)


def ssd_output(ssm_x, b_rows, c_rows, dt_raw, head_vec, seq_ids, prev_id, state_in):
    dt_step, log_cum = head_rates(dt_raw, head_vec)
    row_order = jnp.arange(ssm_x.shape[0])
    linked = (seq_ids[:, None] == seq_ids[None, :]) & (row_order[:, None] >= row_order[None, :])
    log_gaps = log_cum.T[:, :, None] - log_cum.T[:, None, :]
    decays = jnp.exp(jnp.where(linked[None, :, :], log_gaps, -1e30))
    c_dot_b = jnp.dot(c_rows, b_rows.T, precision=PRECISE, preferred_element_type=jnp.float32)
    mixing = decays * c_dot_b[None, :, :] * dt_step.T[:, None, :]
    within = jnp.einsum("hts,shp->thp", mixing, ssm_x, precision=PRECISE)
    carried = jnp.einsum("tn,hpn->thp", c_rows, state_in, precision=PRECISE)
    entry_decay = jnp.exp(log_cum) * (seq_ids == prev_id).astype(jnp.float32)[:, None]
    return within + carried * entry_decay[:, :, None] + head_vec[2][None, :, None] * ssm_x


def ssd_state(ssm_x, b_rows, dt_raw, head_vec, seq_ids, prev_id, state_in):
    dt_step, log_cum = head_rates(dt_raw, head_vec)
    log_last = log_cum[-1]
    same_last = (seq_ids == seq_ids[-1])[:, None]
    tail_decay = jnp.exp(jnp.where(same_last, log_last[None, :] - log_cum, -1e30)) * dt_step
    fresh_state = jnp.einsum("sh,shp,sn->hpn", tail_decay, ssm_x, b_rows, precision=PRECISE)
    through = jnp.exp(log_last) * (seq_ids[-1] == prev_id).astype(jnp.float32)
    return fresh_state + through[:, None, None] * state_in


def block_decay(dt_raw, head_vec, seq_ids, prev_id):
    log_cum = head_rates(dt_raw, head_vec)[1]
    return jnp.exp(log_cum[-1]) * (seq_ids[-1] == prev_id).astype(jnp.float32)


def chain_combine(earlier, later_part):
    return (earlier[0] * later_part[0], later_part[0][:, None, None] * earlier[1] + later_part[1])


def attend_forward(queries, key_rows, value_rows, allowed):
    score_scale = queries.shape[-1] ** (-0.5)
    scores = jnp.dot(queries, key_rows.T, preferred_element_type=jnp.float32) * score_scale
    scores = jnp.where(allowed, scores, -1e30)
    row_max = jnp.max(scores, axis=1, keepdims=True)
    exp_scores = jnp.exp(scores - row_max)
    row_total = jnp.sum(exp_scores, axis=1, keepdims=True)
    attn_prob = (exp_scores / row_total).astype(jnp.bfloat16)
    attended = jnp.dot(attn_prob, value_rows, preferred_element_type=jnp.float32)
    return (attended, row_max[:, 0] + jnp.log(row_total[:, 0]))


def attend_backward(queries, key_rows, value_rows, allowed, lse_rows, grad_rows, delta_rows):
    score_scale = queries.shape[-1] ** (-0.5)
    scores = jnp.dot(queries, key_rows.T, preferred_element_type=jnp.float32) * score_scale
    attn_prob = jnp.exp(jnp.where(allowed, scores, -1e30) - lse_rows[:, None])
    grad_prob = jnp.dot(grad_rows, value_rows.T, preferred_element_type=jnp.float32)
    grad_scores = (attn_prob * (grad_prob - delta_rows[:, None])).astype(jnp.bfloat16)
    grad_q = jnp.dot(grad_scores, key_rows, preferred_element_type=jnp.float32) * score_scale
    grad_k = jnp.dot(grad_scores.T, queries, preferred_element_type=jnp.float32) * score_scale
    grad_v = jnp.dot(
        attn_prob.astype(jnp.bfloat16).T, grad_rows, preferred_element_type=jnp.float32
    )
    return (grad_q, grad_k, grad_v)


def block_shape(num_q, num_kv):
    group_size = num_q // num_kv
    per_block = 2
    return (group_size, per_block, group_size // per_block)


def to_blocks(array, num_blocks):
    moved = jnp.moveaxis(array, 1, 0)
    return moved.reshape((num_blocks, -1) + moved.shape[2:])


def from_blocks(array, group_size, row_count):
    return jnp.moveaxis(array.reshape((group_size, row_count) + array.shape[2:]), 0, 1)


def attention_forward(queries, key_vals, allowed):
    row_count, num_q, head_width = queries.shape
    num_kv = key_vals.shape[1] // 2
    group_size, per_block, num_blocks = block_shape(num_q, num_kv)
    mask_rows = jnp.tile(allowed, (per_block, 1))
    key_rows = key_vals[:, 0]
    value_rows = key_vals[:, num_kv]

    def one_block(q_block):
        return attend_forward(q_block, key_rows, value_rows, mask_rows)

    attn_blocks, lse_blocks = lax.map(one_block, to_blocks(queries, num_blocks))
    out_list = from_blocks(attn_blocks, group_size, row_count)
    lse_list = from_blocks(lse_blocks, group_size, row_count)
    return (out_list, lse_list)


def attention_backward(queries, key_vals, allowed, attn_lse, grad_attn, row_delta):
    row_count, num_q, head_width = queries.shape
    num_kv = key_vals.shape[1] // 2
    group_size, per_block, num_blocks = block_shape(num_q, num_kv)
    mask_rows = jnp.tile(allowed, (per_block, 1))
    key_count = key_vals.shape[0]
    key_rows = key_vals[:, 0]
    value_rows = key_vals[:, num_kv]

    def one_block(sums, block_items):
        q_block, lse_block, grad_block, delta_block = block_items
        grad_q, grad_k, grad_v = attend_backward(
            q_block, key_rows, value_rows, mask_rows, lse_block, grad_block, delta_block
        )
        return ((sums[0] + grad_k, sums[1] + grad_v), grad_q)

    start_sums = (
        jnp.zeros((key_count, head_width), jnp.float32),
        jnp.zeros((key_count, head_width), jnp.float32),
    )
    block_items = (
        to_blocks(queries, num_blocks),
        to_blocks(attn_lse, num_blocks),
        to_blocks(grad_attn, num_blocks),
        to_blocks(row_delta, num_blocks),
    )
    kv_sums, grad_q_blocks = lax.scan(one_block, start_sums, block_items)
    grad_q_list = from_blocks(grad_q_blocks, group_size, row_count)
    grad_k_list = [kv_sums[0][:, None, :]]
    grad_v_list = [kv_sums[1][:, None, :]]
    return (grad_q_list, jnp.concatenate(grad_k_list + grad_v_list, axis=1))


def gather_weights(
    norm_gains,
    mamba_in,
    dt_proj,
    bc_proj,
    mamba_chan,
    bc_conv,
    query_proj,
    kv_proj,
    attn_out,
    mamba_out,
    mlp_in,
    mlp_out,
):
    return (
        lax.all_gather(norm_gains, ("fsdp", "context"), axis=1, tiled=True),
        lax.all_gather(mamba_in, ("fsdp", "context"), axis=0, tiled=True),
        lax.all_gather(dt_proj, ("fsdp", "context"), axis=0, tiled=True),
        lax.all_gather(bc_proj, ("fsdp", "context"), axis=0, tiled=True),
        lax.all_gather(mamba_chan, ("fsdp", "context"), axis=1, tiled=True),
        lax.all_gather(bc_conv, ("fsdp", "context"), axis=1, tiled=True),
        lax.all_gather(query_proj, ("fsdp", "context"), axis=0, tiled=True),
        lax.all_gather(kv_proj, ("fsdp", "context"), axis=0, tiled=True),
        lax.all_gather(attn_out, ("fsdp", "context"), axis=1, tiled=True),
        lax.all_gather(mamba_out, ("fsdp", "context"), axis=1, tiled=True),
        lax.all_gather(mlp_in, ("fsdp", "context"), axis=0, tiled=True),
        lax.all_gather(mlp_out, ("fsdp", "context"), axis=1, tiled=True),
    )


def open_weights(gathered):
    (
        gains_all,
        inner_all,
        step_all,
        state_all,
        chan_all,
        conv_all,
        query_all,
        pair_all,
        attn_all,
        mamba_all,
        mlpin_all,
        mlpout_all,
    ) = gathered
    model_width = inner_all.shape[0]
    conv_taps, conv_bias, norm_gain = unpack_chan(chan_all, conv_all)
    return (
        gains_all[0].astype(jnp.float32),
        gains_all[1].astype(jnp.float32),
        inner_all.reshape(model_width, -1),
        step_all,
        state_all,
        state_all.astype(jnp.float32),
        conv_taps,
        conv_bias,
        norm_gain,
        query_all,
        pair_all.reshape(model_width, -1),
        attn_all,
        mamba_all,
        mlpin_all.reshape(model_width, -1),
        mlpout_all,
    )


def per_device(
    inputs,
    seq_lengths,
    norm_gains,
    mamba_in,
    dt_proj,
    bc_proj,
    mamba_chan,
    bc_conv,
    head_params,
    query_proj,
    kv_proj,
    attn_out,
    mamba_out,
    mlp_in,
    mlp_out,
    out_grad,
):
    local_rows = inputs.shape[0]
    group_rows = local_rows * lax.axis_size("context")
    row_start = lax.axis_index("context") * local_rows
    rim_rows = KCONV - 1
    lengths_row = seq_lengths[0]
    ids_ext, pos_ext = sequence_layout(lengths_row, row_start - rim_rows, local_rows + rim_rows)
    seq_ids = ids_ext[rim_rows:]
    positions = pos_ext[rim_rows:]
    prev_id = ids_ext[rim_rows - 1]
    key_ids = sequence_layout(lengths_row, 0, group_rows)[0]
    query_rows = row_start + jnp.arange(local_rows, dtype=jnp.int32)
    allowed = (key_ids[None, :] == seq_ids[:, None]) & (
        jnp.arange(group_rows, dtype=jnp.int32)[None, :] <= query_rows[:, None]
    )
    num_heads = head_params.shape[1]
    chan_x = num_heads * HDIM
    num_q = query_proj.shape[1] // HDIM
    num_kv = kv_proj.shape[2] // HDIM
    ff_local = mlp_in.shape[2]
    gathered = gather_weights(
        norm_gains,
        mamba_in,
        dt_proj,
        bc_proj,
        mamba_chan,
        bc_conv,
        query_proj,
        kv_proj,
        attn_out,
        mamba_out,
        mlp_in,
        mlp_out,
    )
    (
        gain_mix,
        gain_mlp,
        w_inner,
        w_step,
        w_state,
        w_state32,
        conv_taps,
        conv_bias,
        norm_gain,
        w_query,
        w_pair,
        w_attn,
        w_mamba,
        w_mlpin,
        w_mlpout,
    ) = open_weights(gathered)
    values_in = inputs.astype(jnp.float32)
    normed_one, scale_one = rms_forward(values_in)
    norm_one = (normed_one * gain_mix[None, :]).astype(jnp.bfloat16)
    inner_vals = (
        jnp.dot(norm_one, w_inner, preferred_element_type=jnp.float32)
        .astype(jnp.bfloat16)
        .reshape(local_rows, 2, chan_x)
    )
    z_gate = inner_vals[:, 0].astype(jnp.float32)
    dt_raw = jnp.dot(norm_one, w_step, preferred_element_type=jnp.float32)
    bc_raw = jnp.dot(norm_one, w_state, preferred_element_type=jnp.float32).astype(jnp.bfloat16)
    conv_in = jnp.concatenate([inner_vals[:, 1], bc_raw], axis=1)
    rim_rows_in = from_behind(conv_in[local_rows - rim_rows :], "context", 1)
    extended = jnp.concatenate([rim_rows_in, conv_in], axis=0).astype(jnp.float32)
    pre_act = conv_block(extended, conv_taps, conv_bias, ids_ext)
    activated = jax.nn.silu(pre_act)
    ssm_in = activated[:, :chan_x].reshape(local_rows, num_heads, HDIM)
    state_b = activated[:, chan_x : chan_x + NSTATE]
    state_c = activated[:, chan_x + NSTATE :]
    zero_state = jnp.zeros((num_heads, HDIM, NSTATE), jnp.float32)
    unit_decay = jnp.ones((num_heads,), jnp.float32)
    fresh_state = ssd_state(ssm_in, state_b, dt_raw, head_params, seq_ids, prev_id, zero_state)
    block_fall = block_decay(dt_raw, head_params, seq_ids, prev_id)
    carried = entering(
        (block_fall, fresh_state), "context", chain_combine, (unit_decay, zero_state)
    )
    state_in = carried[1]
    ssm_out = ssd_output(
        ssm_in, state_b, state_c, dt_raw, head_params, seq_ids, prev_id, state_in
    ).reshape(local_rows, chan_x)
    silu_z = jax.nn.silu(z_gate)
    gated_out = ssm_out * silu_z
    sum_squares = jnp.sum(gated_out * gated_out, axis=1)
    norm_in = (gated_out * norm_gain[None, :]).astype(jnp.bfloat16)
    mamba_part = jnp.dot(norm_in, w_mamba, preferred_element_type=jnp.float32)
    cosine, sine = rope_tables(positions, HDIM)
    query_vals = jnp.dot(norm_one, w_query, preferred_element_type=jnp.float32).reshape(
        local_rows, num_q, HDIM
    )
    pair_vals = jnp.dot(norm_one, w_pair, preferred_element_type=jnp.float32).reshape(
        local_rows, 2, num_kv, HDIM
    )
    q_rot = apply_rope(query_vals, cosine, sine).astype(jnp.bfloat16)
    kv_local = jnp.concatenate(
        [apply_rope(pair_vals[:, 0], cosine, sine), pair_vals[:, 1]], axis=1
    ).astype(jnp.bfloat16)
    key_vals = lax.all_gather(
        kv_local.reshape(local_rows, 2 * num_kv * HDIM), "context", axis=0, tiled=True
    ).reshape(group_rows, 2 * num_kv, HDIM)
    attn_vals, attn_lse = attention_forward(q_rot, key_vals, allowed)
    attn_round = attn_vals.astype(jnp.bfloat16)
    attn_flat = attn_round.reshape(local_rows, num_q * HDIM)
    attn_part = jnp.dot(attn_flat, w_attn, preferred_element_type=jnp.float32)
    summed = (
        lax.psum(mamba_part.astype(jnp.bfloat16), "tensor").astype(jnp.float32),
        lax.psum(attn_part.astype(jnp.bfloat16), "tensor").astype(jnp.float32),
        lax.psum(sum_squares.astype(jnp.bfloat16), "tensor").astype(jnp.float32),
    )
    mamba_total = summed[0]
    row_scale = lax.rsqrt(summed[2] / (MH * HDIM) + NORM_EPS)
    residual = values_in + row_scale[:, None] * mamba_total + summed[1]
    normed_two, scale_two = rms_forward(residual)
    norm_two = (normed_two * gain_mlp[None, :]).astype(jnp.bfloat16)
    up_gate = jnp.dot(norm_two, w_mlpin, preferred_element_type=jnp.float32).reshape(
        local_rows, 2, ff_local
    )
    gate_val = up_gate[:, 0]
    up_val = up_gate[:, 1]
    mlp_act = (jax.nn.silu(gate_val) * up_val).astype(jnp.bfloat16)
    down_sum = lax.psum(
        jnp.dot(mlp_act, w_mlpout, preferred_element_type=jnp.float32).astype(jnp.bfloat16),
        "tensor",
    ).astype(jnp.float32)
    output = (residual + down_sum).astype(jnp.bfloat16)
    gathered = gather_weights(
        norm_gains,
        mamba_in,
        dt_proj,
        bc_proj,
        mamba_chan,
        bc_conv,
        query_proj,
        kv_proj,
        attn_out,
        mamba_out,
        mlp_in,
        mlp_out,
    )
    (
        gain_mix,
        gain_mlp,
        w_inner,
        w_step,
        w_state,
        w_state32,
        conv_taps,
        conv_bias,
        norm_gain,
        w_query,
        w_pair,
        w_attn,
        w_mamba,
        w_mlpin,
        w_mlpout,
    ) = open_weights(gathered)
    grad_top = out_grad.astype(jnp.float32)
    grad_act = jnp.dot(out_grad, w_mlpout.T, preferred_element_type=jnp.float32)
    g_mlpout = jnp.dot(mlp_act.T, out_grad, preferred_element_type=jnp.float32)
    grad_upgate = (
        jnp.stack(
            [grad_act * up_val * silu_grad(gate_val), grad_act * jax.nn.silu(gate_val)], axis=1
        )
        .astype(jnp.bfloat16)
        .reshape(local_rows, 2 * ff_local)
    )
    g_mlpin = jnp.dot(norm_two.T, grad_upgate, preferred_element_type=jnp.float32)
    grad_norm_two = lax.psum(
        jnp.dot(grad_upgate, w_mlpin.T, preferred_element_type=jnp.float32).astype(jnp.bfloat16),
        "tensor",
    ).astype(jnp.float32)
    grad_res_two, g_gain_mlp = rms_backward(grad_norm_two, normed_two, scale_two, gain_mlp)
    grad_residual = grad_top + grad_res_two
    grad_round = grad_residual.astype(jnp.bfloat16)
    grad_attn = jnp.dot(grad_round, w_attn.T, preferred_element_type=jnp.float32).reshape(
        local_rows, num_q, HDIM
    )
    g_attnout = jnp.dot(attn_flat.T, grad_round, preferred_element_type=jnp.float32)
    row_delta = jnp.sum(grad_attn * attn_round.astype(jnp.float32), axis=2)
    grad_q, grad_kv_group = attention_backward(
        q_rot, key_vals, allowed, attn_lse, grad_attn.astype(jnp.bfloat16), row_delta
    )
    grad_kv = (
        lax.psum_scatter(
            grad_kv_group.reshape(group_rows, 2 * num_kv * HDIM).astype(jnp.bfloat16),
            "context",
            scatter_dimension=0,
            tiled=True,
        )
        .astype(jnp.float32)
        .reshape(local_rows, 2 * num_kv, HDIM)
    )
    grad_query = (
        undo_rope(grad_q, cosine, sine).astype(jnp.bfloat16).reshape(local_rows, num_q * HDIM)
    )
    grad_pair = (
        jnp.stack([undo_rope(grad_kv[:, :num_kv], cosine, sine), grad_kv[:, num_kv:]], axis=1)
        .astype(jnp.bfloat16)
        .reshape(local_rows, 2 * num_kv * HDIM)
    )
    grad_scaled = (row_scale[:, None] * grad_residual).astype(jnp.bfloat16)
    g_mambaout = jnp.dot(norm_in.T, grad_scaled, preferred_element_type=jnp.float32)
    grad_norm_in = jnp.dot(grad_scaled, w_mamba.T, preferred_element_type=jnp.float32)
    grad_rs = jnp.sum(grad_residual * mamba_total, axis=1)
    g_normgain = jnp.sum(grad_norm_in * gated_out, axis=0)
    grad_gated = (
        grad_norm_in * norm_gain[None, :]
        - gated_out * (grad_rs * row_scale**3 / (MH * HDIM))[:, None]
    )
    grad_ssm = (grad_gated * silu_z).reshape(local_rows, num_heads, HDIM)
    grad_z = grad_gated * ssm_out * silu_grad(z_gate)

    def output_map(ssm_rows, b_rows, c_rows, dt_rows, vec_rows, state_rows):
        return ssd_output(ssm_rows, b_rows, c_rows, dt_rows, vec_rows, seq_ids, prev_id, state_rows)

    def state_map(ssm_rows, b_rows, dt_rows, vec_rows, state_rows):
        return ssd_state(ssm_rows, b_rows, dt_rows, vec_rows, seq_ids, prev_id, state_rows)

    grads_out = jax.vjp(output_map, ssm_in, state_b, state_c, dt_raw, head_params, state_in)[1](
        grad_ssm
    )
    back_carry = entering_2(
        (block_fall, grads_out[5]), "context", chain_combine, (unit_decay, zero_state)
    )
    grads_state = jax.vjp(state_map, ssm_in, state_b, dt_raw, head_params, state_in)[1](
        back_carry[1]
    )
    grad_activated = jnp.concatenate(
        [
            (grads_out[0] + grads_state[0]).reshape(local_rows, chan_x),
            grads_out[1] + grads_state[1],
            grads_out[2],
        ],
        axis=1,
    )
    grad_dt_raw = grads_out[3] + grads_state[2]
    grad_head = grads_out[4] + grads_state[3]
    grad_pre = grad_activated * silu_grad(pre_act)

    def conv_map(ext_rows, taps_in, bias_in):
        return conv_block(ext_rows, taps_in, bias_in, ids_ext)

    grad_ext, g_taps, g_cbias = jax.vjp(conv_map, extended, conv_taps, conv_bias)[1](grad_pre)
    rim_back = from_behind(grad_ext[:rim_rows], "context", -1)
    grad_conv_in = jnp.concatenate(
        [grad_ext[rim_rows:local_rows], grad_ext[local_rows:] + rim_back], axis=0
    )
    grad_inner = (
        jnp.stack([grad_z, grad_conv_in[:, :chan_x]], axis=1)
        .astype(jnp.bfloat16)
        .reshape(local_rows, 2 * chan_x)
    )
    grad_bc = grad_conv_in[:, chan_x:]
    grad_step = grad_dt_raw.astype(jnp.bfloat16)
    g_inner = jnp.dot(norm_one.T, grad_inner, preferred_element_type=jnp.float32)
    g_dt = jnp.dot(norm_one.T, grad_step, preferred_element_type=jnp.float32)
    g_state = jnp.dot(
        norm_one.astype(jnp.float32).T,
        grad_bc,
        precision=PRECISE,
        preferred_element_type=jnp.float32,
    )
    g_query = jnp.dot(norm_one.T, grad_query, preferred_element_type=jnp.float32)
    g_pair = jnp.dot(norm_one.T, grad_pair, preferred_element_type=jnp.float32)
    partial_hn = jnp.dot(grad_inner, w_inner.T, preferred_element_type=jnp.float32)
    partial_hn = partial_hn + jnp.dot(grad_step, w_step.T, preferred_element_type=jnp.float32)
    partial_hn = partial_hn + jnp.dot(grad_query, w_query.T, preferred_element_type=jnp.float32)
    partial_hn = partial_hn + jnp.dot(grad_pair, w_pair.T, preferred_element_type=jnp.float32)
    partial_hn = partial_hn + jnp.dot(
        grad_bc, w_state32.T, precision=PRECISE, preferred_element_type=jnp.float32
    )
    grad_norm_one = lax.psum(partial_hn.astype(jnp.bfloat16), "tensor").astype(jnp.float32)
    grad_res_one, g_gain_mix = rms_backward(grad_norm_one, normed_one, scale_one, gain_mix)
    input_grad = grad_residual + grad_res_one
    chan_grad, conv_grad = pack_chan_grads(g_taps, g_cbias, g_normgain, num_heads)
    model_width = norm_one.shape[1]
    reduced = (
        lax.psum_scatter(
            jnp.stack([g_gain_mix, g_gain_mlp], axis=0),
            ("fsdp", "context"),
            scatter_dimension=1,
            tiled=True,
        ),
        lax.psum_scatter(
            g_inner.reshape(model_width, 2, chan_x),
            ("fsdp", "context"),
            scatter_dimension=0,
            tiled=True,
        ),
        lax.psum_scatter(g_dt, ("fsdp", "context"), scatter_dimension=0, tiled=True),
        lax.psum_scatter(chan_grad, ("fsdp", "context"), scatter_dimension=1, tiled=True),
        lax.psum_scatter(g_query, ("fsdp", "context"), scatter_dimension=0, tiled=True),
        lax.psum_scatter(
            g_pair.reshape(model_width, 2, num_kv * HDIM),
            ("fsdp", "context"),
            scatter_dimension=0,
            tiled=True,
        ),
        lax.psum_scatter(g_attnout, ("fsdp", "context"), scatter_dimension=1, tiled=True),
        lax.psum_scatter(g_mambaout, ("fsdp", "context"), scatter_dimension=1, tiled=True),
        lax.psum_scatter(
            g_mlpin.reshape(model_width, 2, ff_local),
            ("fsdp", "context"),
            scatter_dimension=0,
            tiled=True,
        ),
        lax.psum_scatter(g_mlpout, ("fsdp", "context"), scatter_dimension=1, tiled=True),
    )
    tensor_index = lax.axis_index("tensor")
    head_full = lax.dynamic_update_slice(
        jnp.zeros((3, MH), jnp.float32), grad_head, (0, tensor_index * num_heads)
    )
    shared = lax.psum((head_full, g_state, conv_grad), ("fsdp", "context", "tensor"))
    shard_index = lax.axis_index(("fsdp", "context"))
    shard_count = lax.axis_size(("fsdp", "context"))
    state_rows = model_width // shard_count
    conv_cols = conv_grad.shape[1] // shard_count
    grad_bc_proj = lax.dynamic_slice_in_dim(shared[1], shard_index * state_rows, state_rows, 0)
    grad_bc_conv = lax.dynamic_slice_in_dim(shared[2], shard_index * conv_cols, conv_cols, 1)
    grad_head_params = lax.dynamic_slice_in_dim(shared[0], tensor_index * num_heads, num_heads, 1)
    return (
        output,
        input_grad,
        reduced[0],
        reduced[1],
        reduced[2],
        grad_bc_proj,
        reduced[3],
        grad_bc_conv,
        grad_head_params,
        reduced[4],
        reduced[5],
        reduced[6],
        reduced[7],
        reduced[8],
        reduced[9],
    )


def solution(mesh):
    placed = (
        P(("fsdp", "context"), None),
        P("fsdp", None),
        P(None, ("fsdp", "context")),
        P(("fsdp", "context"), None, "tensor"),
        P(("fsdp", "context"), "tensor"),
        P(("fsdp", "context"), None),
        P("tensor", ("fsdp", "context")),
        P(None, ("fsdp", "context")),
        P(None, "tensor"),
        P(("fsdp", "context"), "tensor"),
        P(("fsdp", "context"), None, "tensor"),
        P("tensor", ("fsdp", "context")),
        P("tensor", ("fsdp", "context")),
        P(("fsdp", "context"), None, "tensor"),
        P("tensor", ("fsdp", "context")),
        P(("fsdp", "context"), None),
    )
    return jax.shard_map(
        per_device,
        mesh=mesh,
        in_specs=placed,
        out_specs=(
            P(("fsdp", "context"), None),
            P(("fsdp", "context"), None),
            P(None, ("fsdp", "context")),
            P(("fsdp", "context"), None, "tensor"),
            P(("fsdp", "context"), "tensor"),
            P(("fsdp", "context"), None),
            P("tensor", ("fsdp", "context")),
            P(None, ("fsdp", "context")),
            P(None, "tensor"),
            P(("fsdp", "context"), "tensor"),
            P(("fsdp", "context"), None, "tensor"),
            P("tensor", ("fsdp", "context")),
            P("tensor", ("fsdp", "context")),
            P(("fsdp", "context"), None, "tensor"),
            P("tensor", ("fsdp", "context")),
        ),
        check_vma=False,
    )
```

profile of v0, /device:TPU:0, one launch (start us, length us, event | category | flops | bytes accessed | tf_op | source)
XLA Modules:
  0.0 1827.8 jit_solution(13381061912786007360)
XLA Ops:
  9.7 43.4 %all-gather.2 = bf16[16,24,12]{1,2,0:T(8,128)(2,1)S(1)} all-gather(bf16[1,24,12]{1,2,0:T(8,128)(2,1)} %bitcast.541), channel_id=1, replica_groups=mesh['fsdp'=4,'context'=4,'tensor'=2] {'fsdp','context'}, dimensions={0}, use_global_device_ids=true | all-gather | bytes 9792 | tf_op jit(solution)/shard_map/all_gather | solution.py:314
  53.3 36.8 %all-gather.3 = bf16[16,16,5]{1,2,0:T(8,128)(2,1)S(1)} all-gather(bf16[1,16,5]{1,2,0:T(8,128)(2,1)} %bitcast.547), channel_id=1, replica_groups=mesh['fsdp'=4,'context'=4,'tensor'=2] {'fsdp','context'}, dimensions={0}, use_global_device_ids=true | all-gather | bytes 2720 | tf_op jit(solution)/shard_map/all_gather | solution.py:315
  95.1 37.2 %all-gather.4 = bf16[16,64,2]{1,2,0:T(2,128)(2,1)S(1)} all-gather(bf16[1,64,2]{1,2,0:T(2,128)(2,1)} %bitcast.551), channel_id=1, replica_groups=mesh['fsdp'=4,'context'=4,'tensor'=2] {'fsdp','context'}, dimensions={0}, use_global_device_ids=true | all-gather | bytes 4352 | tf_op jit(solution)/shard_map/all_gather | solution.py:310
  134.9 36.9 %all-gather.5 = bf16[16,64,12]{1,2,0:T(8,128)(2,1)S(1)} all-gather(bf16[1,64,12]{1,2,0:T(8,128)(2,1)} %bitcast.542), channel_id=1, replica_groups=mesh['fsdp'=4,'context'=4,'tensor'=2] {'fsdp','context'}, dimensions={0}, use_global_device_ids=true | all-gather | bytes 26112 | tf_op jit(solution)/shard_map/all_gather | solution.py:312
  174.9 41.9 %all_gather.73 = bf16[1024,256]{1,0:T(8,128)(2,1)S(1)} all-gather(bf16[64,256]{1,0:T(8,128)(2,1)} %param.30), channel_id=1, replica_groups=mesh['fsdp'=4,'context'=4,'tensor'=2] {'fsdp','context'}, dimensions={0}, use_global_device_ids=true | all-gather | bytes 557056 | tf_op jit(solution)/shard_map/all_gather | solution.py:313
  227.7 42.5 %all_gather.79 = bf16[1024,256]{1,0:T(8,128)(2,1)S(1)} all-gather(bf16[64,256]{1,0:T(8,128)(2,1)S(1)} %copy-done.75), channel_id=1, replica_groups=mesh['fsdp'=4,'context'=4,'tensor'=2] {'fsdp','context'}, dimensions={0}, use_global_device_ids=true | all-gather | bytes 557056 | tf_op jit(solution)/shard_map/all_gather | solution.py:316
  271.6 40.4 %all_gather.80 = bf16[1024,2,64]{2,1,0:T(2,128)(2,1)S(1)} all-gather(bf16[64,2,64]{2,1,0:T(2,128)(2,1)S(1)} %copy-done.76), channel_id=1, replica_groups=mesh['fsdp'=4,'context'=4,'tensor'=2] {'fsdp','context'}, dimensions={0}, use_global_device_ids=true | all-gather | bytes 278528 | tf_op jit(solution)/shard_map/all_gather | solution.py:317
  327.6 41.2 %all_gather.82 = bf16[256,1024]{0,1:T(8,128)(2,1)S(1)} all-gather(bf16[256,64]{0,1:T(8,128)(2,1)S(1)} %copy-done.77), channel_id=1, replica_groups=mesh['fsdp'=4,'context'=4,'tensor'=2] {'fsdp','context'}, dimensions={1}, use_global_device_ids=true | all-gather | bytes 557056 | tf_op jit(solution)/shard_map/all_gather | solution.py:318
  384.9 15.7 all-gather
  427.2 78.9 %all-gather.16.cloned.1.call-done = bf16[1024,2,1024]{2,0,1:T(8,128)(2,1)} async-done(((bf16[64,2,1024]{2,0,1:T(8,128)(2,1)}), bf16[1024,2,1024]{2,0,1:T(8,128)(2,1)}) %all-gather.16.cloned.1.call-update) | async-done | bytes 4194320 | tf_op jit(solution)/shard_map/all_gather | solution.py:320
  517.2 50.6 %all-gather.18.cloned.1.call-done = bf16[1024,1024]{0,1:T(8,128)(2,1)} async-done(((bf16[1024,64]{0,1:T(8,128)(2,1)}), bf16[1024,1024]{0,1:T(8,128)(2,1)}) %all-gather.18.cloned.1.call-update) | async-done | bytes 2097168 | tf_op jit(solution)/shard_map/all_gather | solution.py:321
  603.6 20.3 %all-gather.1 = bf16[48,64,128]{2,1,0:T(8,128)(2,1)} all-gather(bf16[12,64,128]{2,1,0:T(8,128)(2,1)S(1)} %convolution_convert_fusion.4), channel_id=3, replica_groups=mesh['fsdp'=4,'context'=4,'tensor'=2] {'context'}, dimensions={0}, use_global_device_ids=true | all-gather | bytes 983040 | tf_op jit(solution)/shard_map/all_gather | solution.py:48
  639.4 15.7 while.57
  749.3 41.2 %all-reduce.15 = (f32[5,256]{1,0:T(8,128)S(1)}, f32[3,24]{1,0:T(4,128)S(1)}) all-reduce(f32[5,256]{1,0:T(8,128)S(1)} %pad_maximum_fusion.8, f32[3,24]{1,0:T(4,128)S(1)} %dynamic_update_slice.14), channel_id=1, replica_groups=mesh['fsdp'=4,'context'=4,'tensor'=2] {'fsdp','context','tensor'}, use_global_device_ids=true, to_apply=%region_52.54 | all-reduce | flops 1352 | bytes 10816 | tf_op jit(solution)/shard_map/psum | solution.py:690
  790.6 76.4 %all-reduce.14 = f32[12,384]{1,0:T(8,128)S(1)} all-reduce(f32[12,384]{1,0:T(8,128)S(1)} %pad_maximum_fusion.5), channel_id=8, replica_groups=mesh['fsdp'=4,'context'=4,'tensor'=2] {'fsdp','context'}, use_global_device_ids=true, to_apply=%region_51.53.clone | all-reduce | flops 4608 | bytes 36864
  870.4 67.1 %all-reduce.25.cloned.1.call-done = f32[1024,256]{1,0:T(8,128)} async-done(((f32[1024,256]{1,0:T(8,128)}), f32[1024,256]{1,0:T(8,128)}) %all-reduce.25.cloned.1.call-update) | async-done | bytes 1048592 | tf_op jit(solution)/shard_map/psum | solution.py:690
  940.8 76.4 %reduce-scatter.34.cloned.1.call-done = f32[64,2]{1,0:T(8,128)} async-done(((f32[1024,2]{1,0:T(8,128)}), f32[64,2]{1,0:T(8,128)}) %reduce-scatter.34.cloned.1.call-update) | async-done | bytes 528
  1018.6 76.9 %reduce-scatter.22.cloned.1.call-done = f32[64,2,64]{2,0,1:T(8,128)} async-done(((f32[1024,2,64]{2,0,1:T(8,128)}), f32[64,2,64]{2,0,1:T(8,128)}) %reduce-scatter.22.cloned.1.call-update) | async-done | bytes 32784 | tf_op jit(solution)/shard_map/reduce_scatter | solution.py:670
  1097.0 148.2 %reduce-scatter.18.cloned.1.call-done = f32[64,2,768]{2,0,1:T(8,128)} async-done(((f32[1024,2,768]{2,0,1:T(8,128)}), f32[64,2,768]{2,0,1:T(8,128)}) %reduce-scatter.18.cloned.1.call-update) | async-done | bytes 393232 | tf_op jit(solution)/shard_map/reduce_scatter | solution.py:661
  1247.2 179.3 %reduce-scatter.28.cloned.1.call-done = f32[64,2,1024]{2,0,1:T(8,128)} async-done(((f32[1024,2,1024]{2,0,1:T(8,128)}), f32[64,2,1024]{2,0,1:T(8,128)}) %reduce-scatter.28.cloned.1.call-update) | async-done | bytes 524304 | tf_op jit(solution)/shard_map/reduce_scatter | solution.py:678
  1428.7 79.7 %reduce-scatter.20.cloned.1.call-done = f32[64,256]{1,0:T(8,128)} async-done(((f32[1024,256]{1,0:T(8,128)}), f32[64,256]{1,0:T(8,128)}) %reduce-scatter.20.cloned.1.call-update) | async-done | bytes 65552 | tf_op jit(solution)/shard_map/reduce_scatter | solution.py:669
  1508.4 78.9 %reduce-scatter.24.cloned.1.call-done = f32[256,64]{0,1:T(8,128)} async-done(((f32[256,1024]{0,1:T(8,128)}), f32[256,64]{0,1:T(8,128)}) %reduce-scatter.24.cloned.1.call-update) | async-done | bytes 65552 | tf_op jit(solution)/shard_map/reduce_scatter | solution.py:676
  1587.3 134.1 %reduce-scatter.26.cloned.1.call-done = f32[768,64]{0,1:T(8,128)} async-done(((f32[768,1024]{0,1:T(8,128)}), f32[768,64]{0,1:T(8,128)}) %reduce-scatter.26.cloned.1.call-update) | async-done | bytes 196624 | tf_op jit(solution)/shard_map/reduce_scatter | solution.py:677
  1721.4 99.1 %reduce-scatter.30.cloned.1.call-done = f32[1024,64]{0,1:T(8,128)} async-done(((f32[1024,1024]{0,1:T(8,128)}), f32[1024,64]{0,1:T(8,128)}) %reduce-scatter.30.cloned.1.call-update) | async-done | bytes 262160 | tf_op jit(solution)/shard_map/reduce_scatter | solution.py:684
  (535 shorter events, 273.1 us)
Async XLA Ops:
  7.2 362.8 %all-gather.12.cloned.1.call-start = ((), (), s32[]{:S(2)}) async-start(), calls=%async_computation.10 | async-start | bytes 3342336 | tf_op jit(solution)/shard_map/all_gather | solution.py:311
  8.9 396.1 %all-gather.14.cloned.1.call-start = ((), (), s32[]{:S(2)}) async-start(), calls=%async_computation.11 | async-start | bytes 1671168 | tf_op jit(solution)/shard_map/all_gather | solution.py:319
  9.7 416.2 %all-reduce.29.cloned.1.call-start = ((), (), s32[]{:S(2)}) async-start(), calls=%async_computation.27 | async-start | bytes 1048576 | tf_op jit(solution)/shard_map/psum | solution.py:483
  93.8 275.2 %copy-start.96 = (f32[128]{0:T(128)}, f32[128]{0:T(128)S(1)}, u32[]{:S(2)}) copy-start(f32[128]{0:T(128)S(1)} %get-tuple-element.661) | copy-start | bytes 1540
  93.8 288.5 %copy-start.91 = (f32[128]{0:T(128)}, f32[128]{0:T(128)S(1)}, u32[]{:S(2)}) copy-start(f32[128]{0:T(128)S(1)} %get-tuple-element.663) | copy-start | bytes 1540
  93.8 288.5 %copy-start.93 = (f32[128]{0:T(128)}, f32[128]{0:T(128)S(1)}, u32[]{:S(2)}) copy-start(f32[128]{0:T(128)S(1)} %get-tuple-element.664) | copy-start | bytes 1540
  93.8 288.5 %copy-start.95 = (f32[128]{0:T(128)}, f32[128]{0:T(128)S(1)}, u32[]{:S(2)}) copy-start(f32[128]{0:T(128)S(1)} %get-tuple-element.665) | copy-start | bytes 1540
  378.5 3.7 collective-permute-start
  407.9 98.2 %all-gather.16.cloned.1.call-start = ((), (), s32[]{:S(2)}) async-start(), calls=%async_computation.12 | async-start | bytes 4456448 | tf_op jit(solution)/shard_map/all_gather | solution.py:320
  408.8 159.1 %all-gather.18.cloned.1.call-start = ((), (), s32[]{:S(2)}) async-start(), calls=%async_computation.13 | async-start | bytes 2228224 | tf_op jit(solution)/shard_map/all_gather | solution.py:321
  409.3 181.3 %all-reduce.23.cloned.1.call-start = ((), (), s32[]{:S(2)}) async-start(), calls=%async_computation.14 | async-start | bytes 524288 | tf_op jit(solution)/shard_map/psum | solution.py:545
  573.4 128.1 %reduce-scatter.32.cloned.1.call-start = ((), (), s32[]{:S(2)}) async-start(), calls=%async_computation.23 | async-start | bytes 163840
  676.2 15.0 collective-permute-start.1
  681.7 41.3 %all-reduce.27.cloned.1.call-start = ((), (), s32[]{:S(2)}) async-start(), calls=%async_computation.26 | async-start | bytes 1048576 | tf_op jit(solution)/shard_map/psum | solution.py:498
  706.0 162.9 %reduce-scatter.36.cloned.1.call-start = ((), (), s32[]{:S(2)}) async-start(), calls=%async_computation.25 | async-start | bytes 557056
  707.2 230.2 %all-reduce.25.cloned.1.call-start = ((), (), s32[]{:S(2)}) async-start(), calls=%async_computation.16 | async-start | bytes 2097152 | tf_op jit(solution)/shard_map/psum | solution.py:690
  709.1 308.1 %reduce-scatter.34.cloned.1.call-start = ((), (), s32[]{:S(2)}) async-start(), calls=%async_computation.24 | async-start | bytes 557056
  725.3 370.1 %reduce-scatter.22.cloned.1.call-start = ((), (), s32[]{:S(2)}) async-start(), calls=%async_computation.18 | async-start | bytes 1114112 | tf_op jit(solution)/shard_map/reduce_scatter | solution.py:670
  726.8 518.4 %reduce-scatter.18.cloned.1.call-start = ((), (), s32[]{:S(2)}) async-start(), calls=%async_computation.15 | async-start | bytes 6684672 | tf_op jit(solution)/shard_map/reduce_scatter | solution.py:661
  730.9 695.5 %reduce-scatter.28.cloned.1.call-start = ((), (), s32[]{:S(2)}) async-start(), calls=%async_computation.21 | async-start | bytes 8912896 | tf_op jit(solution)/shard_map/reduce_scatter | solution.py:678
  737.0 771.4 %reduce-scatter.20.cloned.1.call-start = ((), (), s32[]{:S(2)}) async-start(), calls=%async_computation.17 | async-start | bytes 1114112 | tf_op jit(solution)/shard_map/reduce_scatter | solution.py:669
  739.1 848.2 %reduce-scatter.24.cloned.1.call-start = ((), (), s32[]{:S(2)}) async-start(), calls=%async_computation.19 | async-start | bytes 1114112 | tf_op jit(solution)/shard_map/reduce_scatter | solution.py:676
  740.6 980.8 %reduce-scatter.26.cloned.1.call-start = ((), (), s32[]{:S(2)}) async-start(), calls=%async_computation.20 | async-start | bytes 3342336 | tf_op jit(solution)/shard_map/reduce_scatter | solution.py:677
  743.1 1077.4 %reduce-scatter.30.cloned.1.call-start = ((), (), s32[]{:S(2)}) async-start(), calls=%async_computation.22 | async-start | bytes 4456448 | tf_op jit(solution)/shard_map/reduce_scatter | solution.py:684
  (111 other events, 3388.5 us)
Sparse Core Ops, SparseCore 0:
  11.3 70.7 all-gather.11
  84.9 56.6 all-gather.13
  408.0 17.7 all-reduce.28
  429.1 76.9 all-gather.15
  508.8 59.0 all-gather.17
  573.6 17.0 all-reduce.22
  681.9 19.6 reduce-scatter.31
  706.1 16.8 all-reduce.26
  725.8 79.1 reduce-scatter.35
  810.1 127.3 all-reduce.24
  940.3 76.7 reduce-scatter.33
  1019.3 76.1 reduce-scatter.21
  1100.7 144.4 reduce-scatter.17
  1247.3 179.1 reduce-scatter.27
  1429.2 79.1 reduce-scatter.19
  1511.1 76.2 reduce-scatter.23
  1592.7 128.6 reduce-scatter.25
  1724.1 96.3 reduce-scatter.29
where the time goes:
time: 1840 us; the launch traced here: 1830 us
  waiting for transfers between devices  1120 us (61%)
  blocking collectives  496 us (27%)
  matrix products  84.2 us (5%)
  local copies, waits for them, and re-layouts  57.5 us (3%)
  other arithmetic  45.1 us (2%)
  between operations  18.8 us (1%)
    reduce_scatter x1, waiting for transfers between devices, per_device(): lax.psum_scatter(g_mlpin.reshape(model_width, 2, ff_local), ('fsdp', 'con...  179 us
    reduce_scatter x1, waiting for transfers between devices, per_device(): lax.psum_scatter(g_inner.reshape(model_width, 2, chan_x), ('fsdp', 'conte...  148 us
    reduce_scatter x1, waiting for transfers between devices, per_device(): lax.psum_scatter(g_mambaout, ('fsdp', 'context'), scatter_dimension=1, ti...  134 us
    reduce_scatter x1, waiting for transfers between devices, per_device(): lax.psum_scatter(g_mlpout, ('fsdp', 'context'), scatter_dimension=1, tile...  99.1 us
    unnamed x21, waiting for transfers between devices  86 us
    reduce_scatter x1, waiting for transfers between devices, per_device(): lax.psum_scatter(g_query, ('fsdp', 'context'), scatter_dimension=0, tiled...  79.7 us
    reduce_scatter x1, waiting for transfers between devices, per_device(): lax.psum_scatter(g_attnout, ('fsdp', 'context'), scatter_dimension=1, til...  78.9 us
    all_gather x1, waiting for transfers between devices, gather_weights(): lax.all_gather(mlp_in, ('fsdp', 'context'), axis=0, tiled=True)  78.9 us
  transfers between devices with their start and end apart: 20, of which 16 were waited for; matrix products, arithmetic and copies ran while one was open for 6% of the time, Pallas kernels for 0%

commit v1 on v0

v1 whole, which is shorter than its diff:
```python
import jax
import jax.numpy as jnp
from jax import lax
from jax.sharding import PartitionSpec as P

HDIM = 64
NSTATE = 128
KCONV = 4
NORM_EPS = 1e-05
ROPE_BASE = 100000000000.0
EXACT = lax.Precision.HIGHEST
BF = jnp.bfloat16
F32 = jnp.float32


def swap_pair(block):
    return lax.ppermute(block, "tensor", [(0, 1), (1, 0)])


def join_pair(own, other, place, axis):
    low = jnp.where(place == 0, own, other)
    high = jnp.where(place == 0, other, own)
    return jnp.stack([low, high], axis=axis)


def exchange(blocks, axis):
    return lax.all_to_all(blocks, axis, 0, 0, tiled=True)


def spread(block, axis):
    return exchange(jnp.broadcast_to(block[None], (lax.axis_size(axis),) + block.shape), axis)


def hops(axis):
    count = lax.axis_size(axis)
    place = lax.axis_index(axis)
    for step in range(1, count):
        route = [(i, (i + step) % count) for i in range(count)]
        yield route, (place + step) % count, (place - step) % count


def spread_async(block, axis):
    count = lax.axis_size(axis)
    whole = jnp.zeros((count,) + block.shape, block.dtype)
    whole = lax.dynamic_update_index_in_dim(whole, block, lax.axis_index(axis), 0)
    for route, _, source in hops(axis):
        whole = lax.dynamic_update_index_in_dim(whole, lax.ppermute(block, axis, route), source, 0)
    return whole


def reduce_async(blocks, axis):
    total = lax.dynamic_index_in_dim(blocks, lax.axis_index(axis), 0, False).astype(F32)
    for route, target, _ in hops(axis):
        sent = lax.dynamic_index_in_dim(blocks, target, 0, False)
        total = total + lax.ppermute(sent, axis, route).astype(F32)
    return total


def sigmoid(values):
    return 1.0 / (1.0 + jnp.exp(-values))


def silu_grad(values, sigma):
    return sigma * (1.0 + values * (1.0 - sigma))


def rms_forward(values):
    inv_rms = lax.rsqrt(jnp.mean(values * values, axis=-1, keepdims=True) + NORM_EPS)
    return values * inv_rms, inv_rms


def rms_backward(grad_out, normed, inv_rms, gain_vec):
    grad_normed = grad_out * gain_vec[None, :]
    return inv_rms * (grad_normed - normed * jnp.mean(grad_normed * normed, axis=-1, keepdims=True))


def rotate_half(values):
    width = values.shape[-1] // 2
    return jnp.concatenate([-values[..., width:], values[..., :width]], axis=-1)


def dot(left, right, exact=None):
    return lax.dot_general(
        left, right, (((1,), (0,)), ((), ())), precision=exact, preferred_element_type=F32
    )


def dot_nt(left, right, exact=None):
    return lax.dot_general(
        left, right, (((1,), (1,)), ((), ())), precision=exact, preferred_element_type=F32
    )


def dot_tn(left, right, exact=None):
    return lax.dot_general(
        left, right, (((0,), (0,)), ((), ())), precision=exact, preferred_element_type=F32
    )


def pad_to(array, axis, size):
    if array.shape[axis] == size:
        return array
    widths = [(0, 0)] * array.ndim
    widths[axis] = (0, size - array.shape[axis])
    return jnp.pad(array, widths)


def ceil_to(value, unit):
    return -(-value // unit) * unit


def per_device(
    inputs,
    seq_lengths,
    norm_gains,
    mamba_in,
    dt_proj,
    bc_proj,
    mamba_chan,
    bc_conv,
    head_params,
    query_proj,
    kv_proj,
    attn_out,
    mamba_out,
    mlp_in,
    mlp_out,
    out_grad,
):
    n_f = lax.axis_size("fsdp")
    n_c = lax.axis_size("context")
    c_id = lax.axis_index("context")
    t_id = lax.axis_index("tensor")
    shards = n_f * n_c
    rows = inputs.shape[0]
    group = rows * n_c
    half = rows // 2
    d_loc = mamba_in.shape[0]
    width = d_loc * shards
    heads_t = head_params.shape[1]
    heads = -(-heads_t // n_c)
    heads_pad = heads * n_c
    q_t = query_proj.shape[1] // HDIM
    qh = -(-q_t // n_c)
    q_pad = qh * n_c
    kv_w = kv_proj.shape[2]
    ff = mlp_in.shape[2]
    chan = heads * HDIM
    chan_total = heads_t * HDIM * 2
    q_w = qh * HDIM
    bc_w = 2 * NSTATE
    conv_w = chan + bc_w
    o_x = chan
    o_q = chan + conv_w
    o_k = o_q + q_w
    o_v = o_k + kv_w
    o_dt = o_v + kv_w
    a_w = ceil_to(o_dt + heads, 128)
    cc = bc_conv.shape[1]
    mc = mamba_chan.shape[1]

    chan_ctx = pad_to(mamba_chan, 0, heads_pad).reshape(n_c, heads * mc)
    common = jnp.concatenate([norm_gains.reshape(-1), bc_conv.reshape(-1)])
    small = jnp.concatenate(
        [jnp.broadcast_to(common[None], (n_c,) + common.shape), chan_ctx], axis=1
    )
    s_len = small.shape[1]
    small = pad_to(small, 1, ceil_to(s_len, 128))
    small = exchange(small, "context")
    small = spread(small, "fsdp").reshape(shards, -1).astype(F32)
    n_gain = 2 * d_loc
    n_conv = (KCONV + 1) * cc
    gains = jnp.transpose(small[:, :n_gain].reshape(shards, 2, d_loc), (1, 0, 2)).reshape(2, width)
    conv_bc = jnp.transpose(
        small[:, n_gain : n_gain + n_conv].reshape(shards, KCONV + 1, cc), (1, 0, 2)
    ).reshape(KCONV + 1, bc_w)
    chan_all = jnp.transpose(
        small[:, n_gain + n_conv : s_len].reshape(shards, heads, mc), (1, 0, 2)
    ).reshape(heads, KCONV + 2, HDIM)
    chan_all = jnp.transpose(chan_all, (1, 0, 2)).reshape(KCONV + 2, chan)
    gain_mix = gains[0]
    gain_mlp = gains[1]
    conv_all = jnp.concatenate([chan_all[: KCONV + 1], conv_bc], axis=1)
    norm_gain = chan_all[KCONV + 1]

    inner_ctx = pad_to(mamba_in.reshape(d_loc, 2, heads_t, HDIM), 2, heads_pad)
    inner_ctx = jnp.transpose(inner_ctx.reshape(d_loc, 2, n_c, chan), (2, 0, 1, 3))
    query_ctx = jnp.transpose(
        pad_to(query_proj, 1, q_pad * HDIM).reshape(d_loc, n_c, q_w), (1, 0, 2)
    )
    dt_ctx = jnp.transpose(pad_to(dt_proj, 1, heads_pad).reshape(d_loc, n_c, heads), (1, 0, 2))
    bc_ctx = jnp.broadcast_to(bc_proj[None], (n_c, d_loc, bc_w))
    kv_ctx = jnp.broadcast_to(kv_proj.reshape(1, d_loc, 2 * kv_w), (n_c, d_loc, 2 * kv_w))
    pack_a = pad_to(
        jnp.concatenate(
            [inner_ctx.reshape(n_c, d_loc, 2 * chan), bc_ctx, query_ctx, kv_ctx, dt_ctx], axis=2
        ),
        2,
        a_w,
    )
    mo_ctx = jnp.swapaxes(pad_to(mamba_out, 0, heads_pad * HDIM).reshape(n_c, chan, d_loc), 1, 2)
    ao_ctx = jnp.swapaxes(pad_to(attn_out, 0, q_pad * HDIM).reshape(n_c, q_w, d_loc), 1, 2)
    pack_b = jnp.concatenate([mo_ctx, ao_ctx], axis=2)
    b_w = chan + q_w

    mine = lax.dynamic_slice_in_dim(inputs, t_id * half, half, 0)

    part_a = exchange(pack_a, "context").reshape(n_c * d_loc, a_w)
    w_a = spread(part_a, "fsdp").reshape(width, a_w)
    got_in = exchange(jnp.broadcast_to(mine[None], (n_c,) + mine.shape), "context")
    rows_in = join_pair(got_in, swap_pair(got_in), t_id, 1).reshape(group, width)
    part_b = exchange(pack_b, "context").reshape(n_c * d_loc, b_w)
    w_b = spread(part_b, "fsdp").reshape(width, b_w)

    mlp_in_flat = mlp_in.reshape(d_loc, 2 * ff)
    mlp_out_t = mlp_out.T
    mlp_in_flat, mlp_out_t, _ = lax.optimization_barrier((mlp_in_flat, mlp_out_t, part_b))
    mlp_in_part = spread_async(mlp_in_flat, "context").reshape(n_c * d_loc, 2 * ff)
    mlp_out_part = spread_async(mlp_out_t, "context").reshape(n_c * d_loc, ff)
    w_mi = spread_async(mlp_in_part, "fsdp").reshape(width, 2 * ff)
    w_mo = spread_async(mlp_out_part, "fsdp").reshape(width, ff)

    lengths_row = seq_lengths[0]
    starts = jnp.cumsum(lengths_row) - lengths_row
    row_ids = jnp.arange(group, dtype=jnp.int32)
    inside = row_ids[:, None] >= starts[None, :]
    seq_ids = jnp.sum(inside.astype(jnp.int32), axis=1) - 1
    positions = row_ids - jnp.max(jnp.where(inside, starts[None, :], 0), axis=1)
    linked = (seq_ids[:, None] == seq_ids[None, :]) & (row_ids[:, None] >= row_ids[None, :])

    head_vec = lax.dynamic_slice_in_dim(
        pad_to(head_params, 1, heads_pad), c_id * heads, heads, 1
    )

    normed_one = rms_forward(rows_in.astype(F32))[0]
    norm_one = (normed_one * gain_mix[None, :]).astype(BF)
    proj = dot(norm_one, w_a)
    z_gate = proj[:, :chan].astype(BF).astype(F32)
    conv_in = proj[:, o_x:o_q].astype(BF).astype(F32)
    dt_raw = proj[:, o_dt : o_dt + heads]

    def behind(values, step):
        moved = jnp.pad(values, ((step, 0), (0, 0)))[:group]
        return jnp.where((positions >= step)[:, None], moved, 0.0)

    def ahead(values, step):
        kept = jnp.where((positions >= step)[:, None], values, 0.0)
        return jnp.pad(kept, ((0, step), (0, 0)))[step:]

    pre_act = conv_all[KCONV][None, :]
    for k in range(KCONV):
        pre_act = pre_act + conv_all[k][None, :] * behind(conv_in, KCONV - 1 - k)
    pre_sig = sigmoid(pre_act)
    activated = pre_act * pre_sig
    ssm_x = activated[:, :chan]
    state_b = activated[:, chan : chan + NSTATE].astype(BF)
    state_c = activated[:, chan + NSTATE :].astype(BF)
    dt_step = jax.nn.softplus(dt_raw + head_vec[0][None, :])
    rate = jnp.exp(head_vec[1])[None, :]
    decay_log = -dt_step * rate
    lower = (row_ids[:, None] >= row_ids[None, :]).astype(F32)
    log_cum = dot(lower, decay_log, EXACT)
    cum_t = log_cum.T
    dt_t = dt_step.T
    c_dot_b = dot_nt(state_c, state_b)
    ssm_list = []
    for j in range(heads):
        gaps = jnp.where(linked, log_cum[:, j : j + 1] - cum_t[j : j + 1], -1e30)
        mixing = jnp.exp(gaps) * c_dot_b * dt_t[j : j + 1]
        x_head = ssm_x[:, j * HDIM : (j + 1) * HDIM]
        core = dot(mixing.astype(BF), x_head.astype(BF))
        ssm_list.append(core + head_vec[2, j] * x_head)
    ssm_out = jnp.concatenate(ssm_list, axis=1)
    z_sig = sigmoid(z_gate)
    silu_z = z_gate * z_sig
    gated = ssm_out * silu_z
    squares = jnp.sum(gated * gated, axis=1).reshape(n_c, rows)
    norm_in = (gated * norm_gain[None, :]).astype(BF)
    mamba_part = dot_nt(norm_in, w_b[:, :chan])

    freqs = jnp.power(ROPE_BASE, -jnp.arange(HDIM // 2).astype(F32) * (2.0 / HDIM))
    angles = positions.astype(F32)[:, None] * freqs[None, :]
    angles = jnp.concatenate([angles, angles], axis=1)
    cosine = jnp.cos(angles)
    sine = jnp.sin(angles)
    scale = HDIM ** (-0.5)
    k_raw = proj[:, o_k : o_k + HDIM]
    k_rot = (k_raw * cosine + rotate_half(k_raw) * sine).astype(BF)
    v_rows = proj[:, o_v : o_v + HDIM].astype(BF)
    q_list = []
    val_list = []
    prob_list = []
    for j in range(qh):
        q_raw = proj[:, o_q + j * HDIM : o_q + (j + 1) * HDIM]
        q_rot = (q_raw * cosine + rotate_half(q_raw) * sine).astype(BF)
        scores = jnp.where(linked, dot_nt(q_rot, k_rot) * scale, -1e30)
        exps = jnp.exp(scores - jnp.max(scores, axis=1, keepdims=True))
        probs = exps / jnp.sum(exps, axis=1, keepdims=True)
        probs_round = probs.astype(BF)
        q_list.append(q_rot)
        prob_list.append(probs_round)
        val_list.append(dot(probs_round, v_rows).astype(BF))
    attn_flat = jnp.concatenate(val_list, axis=1)
    attn_part = dot_nt(attn_flat, w_b[:, chan:])

    def pair_sum(values, lead):
        parts = values.reshape(lead + (2, half) + values.shape[1:])
        axis = len(lead)
        keep = lax.dynamic_index_in_dim(parts, t_id, axis, False)
        give = lax.dynamic_index_in_dim(parts, 1 - t_id, axis, False).astype(BF)
        return keep + swap_pair(give).astype(F32)

    both = jnp.concatenate([mamba_part, attn_part], axis=1)
    both = pair_sum(both, (n_c,)).astype(BF)
    both = jnp.sum(exchange(both, "context").astype(F32), axis=0)
    squares = squares + swap_pair(squares)
    squares = jnp.sum(spread(squares, "context"), axis=0)
    scale_rows = lax.rsqrt(squares / chan_total + NORM_EPS)
    scale_own = lax.dynamic_slice(scale_rows, (c_id, t_id * half), (1, half)).reshape(half, 1)
    scale_all = scale_rows.reshape(group, 1)
    mamba_own = both[:, :width]
    in_own = mine.astype(F32)
    residual = in_own + scale_own * mamba_own + both[:, width:]

    normed_two, inv_two = rms_forward(residual)
    norm_two_own = (normed_two * gain_mlp[None, :]).astype(BF)
    norm_two = join_pair(norm_two_own, swap_pair(norm_two_own), t_id, 0).reshape(rows, width)
    up_gate = dot(norm_two, w_mi)
    gate_val = up_gate[:, :ff]
    up_val = up_gate[:, ff:]
    gate_sig = sigmoid(gate_val)
    gate_act = gate_val * gate_sig
    mlp_act = (gate_act * up_val).astype(BF)
    grad_act = dot(out_grad, w_mo)
    grad_gate = (grad_act * up_val * silu_grad(gate_val, gate_sig)).astype(BF)
    grad_up = (grad_act * gate_act).astype(BF)
    grad_upgate = jnp.concatenate([grad_gate, grad_up], axis=1)
    grad_two = pair_sum(dot_nt(grad_upgate, w_mi), ())
    down_own = pair_sum(dot_nt(mlp_act, w_mo), ())
    out_own = (residual + down_own).astype(BF)
    output = join_pair(out_own, swap_pair(out_own), t_id, 0).reshape(rows, width)
    g_mi = dot_tn(norm_two, grad_upgate).astype(BF)
    g_mo = dot_tn(out_grad, mlp_act).astype(BF)

    top_own = lax.dynamic_slice_in_dim(out_grad, t_id * half, half, 0).astype(F32)
    g_gain_mlp = jnp.sum(grad_two * normed_two, axis=0)
    grad_res = top_own + rms_backward(grad_two, normed_two, inv_two, gain_mlp)
    grad_rs_own = jnp.sum(grad_res * mamba_own, axis=1)
    got_rs = spread(grad_rs_own.reshape(1, half), "context")
    grad_rs = join_pair(got_rs, swap_pair(got_rs), t_id, 1).reshape(group, 1)
    got_res = exchange(
        jnp.broadcast_to(grad_res.astype(BF)[None], (n_c, half, width)), "context"
    )
    grad_round = join_pair(got_res, swap_pair(got_res), t_id, 1).reshape(group, width)
    grad_scaled = (grad_round.astype(F32) * scale_all).astype(BF)

    def reduce_weight(grad, use):
        cols = grad.shape[1]
        blocks = grad.reshape(n_f, n_c * d_loc, cols)
        return use(blocks, "fsdp").astype(BF).reshape(n_c, d_loc, cols)

    def sum_exchange(blocks, axis):
        return jnp.sum(exchange(blocks, axis).astype(F32), axis=0)

    g_mi, g_mo, grad_round = lax.optimization_barrier((g_mi, g_mo, grad_round))
    out_mi = reduce_async(reduce_weight(g_mi, reduce_async), "context").reshape(d_loc, 2, ff)
    out_mo = reduce_async(reduce_weight(g_mo, reduce_async), "context").T

    g_b = jnp.concatenate([dot_tn(grad_scaled, norm_in), dot_tn(grad_round, attn_flat)], axis=1)
    g_b = reduce_weight(g_b.astype(BF), sum_exchange)
    g_b = exchange(g_b, "context").astype(F32)
    out_mout = jnp.swapaxes(g_b[:, :, :chan], 1, 2).reshape(heads_pad * HDIM, d_loc)
    out_mout = out_mout[: heads_t * HDIM]
    out_aout = jnp.swapaxes(g_b[:, :, chan:], 1, 2).reshape(q_pad * HDIM, d_loc)
    out_aout = out_aout[: q_t * HDIM]

    grad_attn = dot(grad_round, w_b[:, chan:])
    grad_k = jnp.zeros((group, HDIM), F32)
    grad_v = jnp.zeros((group, HDIM), F32)
    grad_q_list = []
    for j in range(qh):
        part = slice(j * HDIM, (j + 1) * HDIM)
        g_attn = grad_attn[:, part]
        delta = jnp.sum(g_attn * val_list[j].astype(F32), axis=1, keepdims=True)
        g_attn = g_attn.astype(BF)
        grad_prob = dot_nt(g_attn, v_rows)
        g_scores = (prob_list[j].astype(F32) * (grad_prob - delta)).astype(BF)
        g_q = dot(g_scores, k_rot) * scale
        grad_k = grad_k + dot_tn(g_scores, q_list[j]) * scale
        grad_v = grad_v + dot_tn(prob_list[j], g_attn)
        grad_q_list.append((g_q * cosine - rotate_half(g_q) * sine).astype(BF))
    grad_k = (grad_k * cosine - rotate_half(grad_k) * sine).astype(BF)
    grad_v = grad_v.astype(BF)

    grad_norm_in = dot(grad_scaled, w_b[:, :chan])
    g_norm_gain = jnp.sum(grad_norm_in * gated, axis=0)
    grad_gated = grad_norm_in * norm_gain[None, :] - gated * (
        grad_rs * scale_all * scale_all * scale_all / chan_total
    )
    grad_ssm = grad_gated * silu_z
    grad_z = (grad_gated * ssm_out * silu_grad(z_gate, z_sig)).astype(BF)

    grad_cb = jnp.zeros((group, group), F32)
    grad_x_list = []
    row_list = []
    col_list = []
    skip_list = []
    for j in range(heads):
        part = slice(j * HDIM, (j + 1) * HDIM)
        gaps = jnp.where(linked, log_cum[:, j : j + 1] - cum_t[j : j + 1], -1e30)
        decays = jnp.exp(gaps)
        weights = decays * c_dot_b
        x_head = ssm_x[:, part]
        g_head = grad_ssm[:, part]
        g_round = g_head.astype(BF)
        grad_mix = dot_nt(g_round, x_head.astype(BF))
        grad_x_list.append(
            dot_tn((weights * dt_t[j : j + 1]).astype(BF), g_round) + head_vec[2, j] * g_head
        )
        grad_cb = grad_cb + grad_mix * decays * dt_t[j : j + 1]
        flow = grad_mix * weights
        col_list.append(jnp.sum(flow, axis=0))
        row_list.append(jnp.sum(flow * dt_t[j : j + 1], axis=1))
        skip_list.append(jnp.sum(g_head * x_head))
    grad_cb = grad_cb.astype(BF)
    grad_c = dot(grad_cb, state_b)
    grad_b = dot_tn(grad_cb, state_c)
    col_sum = jnp.stack(col_list, axis=1)
    grad_cum = jnp.stack(row_list, axis=1) - dt_step * col_sum
    grad_decay = dot_tn(lower, grad_cum, EXACT)
    grad_dt = col_sum - rate * grad_decay
    grad_dt_raw = grad_dt * sigmoid(dt_raw + head_vec[0][None, :])
    g_head_params = jnp.stack(
        [
            jnp.sum(grad_dt_raw, axis=0),
            jnp.sum(grad_decay * decay_log, axis=0),
            jnp.stack(skip_list),
        ]
    )

    grad_act_mix = jnp.concatenate(grad_x_list + [grad_b, grad_c], axis=1)
    grad_pre = grad_act_mix * silu_grad(pre_act, pre_sig)
    grad_conv = jnp.zeros_like(grad_pre)
    g_taps = []
    for k in range(KCONV):
        step = KCONV - 1 - k
        g_taps.append(jnp.sum(grad_pre * behind(conv_in, step), axis=0))
        grad_conv = grad_conv + conv_all[k][None, :] * ahead(grad_pre, step)
    g_taps.append(jnp.sum(grad_pre, axis=0))
    g_taps = jnp.stack(g_taps)

    grad_a = pad_to(
        jnp.concatenate(
            [grad_z, grad_conv.astype(BF)]
            + grad_q_list
            + [pad_to(grad_k, 1, kv_w), pad_to(grad_v, 1, kv_w), grad_dt_raw.astype(BF)],
            axis=1,
        ),
        1,
        a_w,
    )
    partial = dot_nt(grad_a, w_a)
    g_gain_mix = jnp.sum(partial * normed_one, axis=0)
    partial = pair_sum(partial, (n_c,)).astype(BF)
    grad_one = jnp.sum(exchange(partial, "context").astype(F32), axis=0)
    normed_own, inv_own = rms_forward(in_own)
    grad_in_own = grad_res + rms_backward(grad_one, normed_own, inv_own, gain_mix)
    input_grad = join_pair(grad_in_own, swap_pair(grad_in_own), t_id, 0).reshape(rows, width)

    g_a = reduce_weight(dot_tn(norm_one, grad_a).astype(BF), sum_exchange)
    g_a = exchange(g_a, "context").astype(F32)
    out_inner = jnp.transpose(g_a[:, :, : 2 * chan].reshape(n_c, d_loc, 2, chan), (1, 2, 0, 3))
    out_inner = out_inner.reshape(d_loc, 2, heads_pad * HDIM)[:, :, : heads_t * HDIM]
    out_query = jnp.swapaxes(g_a[:, :, o_q:o_k], 0, 1).reshape(d_loc, q_pad * HDIM)
    out_query = out_query[:, : q_t * HDIM]
    out_dt = jnp.swapaxes(g_a[:, :, o_dt : o_dt + heads], 0, 1).reshape(d_loc, heads_pad)
    out_dt = out_dt[:, :heads_t]
    out_kv = jnp.sum(g_a[:, :, o_k:o_dt], axis=0).reshape(d_loc, 2, kv_w)
    sum_bc = jnp.sum(g_a[:, :, o_x + chan : o_q], axis=0)

    g_gains = jnp.stack([g_gain_mix, g_gain_mlp]).reshape(2, shards, d_loc)
    g_gains = jnp.transpose(g_gains, (1, 0, 2)).reshape(shards, n_gain)
    g_convbc = jnp.transpose(
        g_taps[:, chan:].reshape(KCONV + 1, shards, cc), (1, 0, 2)
    ).reshape(shards, n_conv)
    g_chan = jnp.concatenate([g_taps[:, :chan], g_norm_gain[None]], axis=0)
    g_chan = jnp.transpose(g_chan.reshape(KCONV + 2, heads, HDIM), (1, 0, 2))
    g_chan = jnp.transpose(g_chan.reshape(heads, shards, mc), (1, 0, 2)).reshape(shards, heads * mc)
    g_heads = jnp.broadcast_to(g_head_params.reshape(1, -1), (shards, 3 * heads))
    g_small = jnp.concatenate([g_gains, g_convbc, g_chan, g_heads], axis=1)
    g_len = g_small.shape[1]
    g_small = pad_to(g_small, 1, ceil_to(g_len, 128)).reshape(n_f, n_c, -1)
    g_small = jnp.sum(exchange(g_small, "fsdp"), axis=0)
    g_small = exchange(g_small, "context")
    g_common = jnp.sum(g_small[:, : n_gain + n_conv], axis=0)
    tail = jnp.concatenate([sum_bc.reshape(-1), g_common])
    tail = tail + swap_pair(tail)
    out_bc = tail[: d_loc * bc_w].reshape(d_loc, bc_w)
    g_common = tail[d_loc * bc_w :]
    out_gains = g_common[:n_gain].reshape(2, d_loc)
    out_convbc = g_common[n_gain:].reshape(KCONV + 1, cc)
    out_chan = g_small[:, n_gain + n_conv : n_gain + n_conv + heads * mc]
    out_chan = out_chan.reshape(heads_pad, mc)[:heads_t]
    out_heads = g_small[:, n_gain + n_conv + heads * mc : g_len].reshape(n_c, 3, heads)
    out_heads = jnp.swapaxes(out_heads, 0, 1).reshape(3, heads_pad)[:, :heads_t]

    return (
        output,
        input_grad,
        out_gains,
        out_inner,
        out_dt,
        out_bc,
        out_chan,
        out_convbc,
        out_heads,
        out_query,
        out_kv,
        out_aout,
        out_mout,
        out_mi,
        out_mo,
    )


def solution(mesh):
    both = ("fsdp", "context")
    rows = P(both, None)
    return jax.shard_map(
        per_device,
        mesh=mesh,
        in_specs=(
            rows,
            P("fsdp", None),
            P(None, both),
            P(both, None, "tensor"),
            P(both, "tensor"),
            rows,
            P("tensor", both),
            P(None, both),
            P(None, "tensor"),
            P(both, "tensor"),
            P(both, None, "tensor"),
            P("tensor", both),
            P("tensor", both),
            P(both, None, "tensor"),
            P("tensor", both),
            rows,
        ),
        out_specs=(
            rows,
            rows,
            P(None, both),
            P(both, None, "tensor"),
            P(both, "tensor"),
            rows,
            P("tensor", both),
            P(None, both),
            P(None, "tensor"),
            P(both, "tensor"),
            P(both, None, "tensor"),
            P("tensor", both),
            P("tensor", both),
            P(both, None, "tensor"),
            P("tensor", both),
        ),
        check_vma=False,
    )
```

time: 1840 us -> 496 us (0.27)
  waiting for transfers between devices: 1120 us -> 137 us
  blocking collectives: 496 us -> 0 us
  starting transfers between devices: 4.63 us -> 131 us
  local copies, waits for them, and re-layouts: 57.5 us -> 98.8 us
  matrix products: 84.2 us -> 60.2 us
    reduce_scatter x7 -> x0, waiting for transfers between devices: 796 us -> none  [the longest x1 179 us: per_device(): lax.psum_scatter(g_mlpin.reshape(model_width, 2, ff_local), ('fsdp', 'con...]
    all_gather x12 -> x0, blocking collectives: 376 us -> none  [the longest x1 43.4 us: gather_weights(): lax.all_gather(mamba_chan, ('fsdp', 'context'), axis=1, tiled=True)]
    all_gather x4 -> x0, waiting for transfers between devices: 130 us -> none  [the longest x1 78.9 us: gather_weights(): lax.all_gather(mlp_in, ('fsdp', 'context'), axis=0, tiled=True)]
    psum x4 -> x0, waiting for transfers between devices: 109 us -> none  [the longest x1 67.1 us: per_device(): lax.psum((head_full, g_state, conv_grad), ('fsdp', 'context', 'tensor'))]
    unnamed x21 -> x0, waiting for transfers between devices: 86 us -> none
    unnamed x1 -> x0, blocking collectives: 76.4 us -> none
    all_to_all x0 -> x18, starting transfers between devices: none -> 76.2 us  [exchange(): return lax.all_to_all(blocks, axis, 0, 0, tiled=True)]
    all_to_all x0 -> x18, waiting for transfers between devices: none -> 74.1 us  [exchange(): return lax.all_to_all(blocks, axis, 0, 0, tiled=True)]
  transfers between devices with their start and end apart: 20 -> 54, of which waited for: 16 -> 18; matrix products, arithmetic and copies ran while one was open for 6% -> 28% of each run, Pallas kernels for 0% -> 0%
where the time goes in v1:
time: 496 us; the launch traced here: 488 us
  waiting for transfers between devices  137 us (28%)
  starting transfers between devices  131 us (26%)
  local copies, waits for them, and re-layouts  98.8 us (20%)
  matrix products  60.2 us (12%)
  other arithmetic  59.2 us (12%)
    all_to_all x18, starting transfers between devices, exchange(): return lax.all_to_all(blocks, axis, 0, 0, tiled=True)  76.2 us
    all_to_all x18, waiting for transfers between devices, exchange(): return lax.all_to_all(blocks, axis, 0, 0, tiled=True)  74.1 us
    ppermute x12, waiting for transfers between devices, reduce_async(): total = total + lax.ppermute(sent, axis, route).astype(F32)  42.6 us
    ppermute x12, starting transfers between devices, reduce_async(): total = total + lax.ppermute(sent, axis, route).astype(F32)  30.7 us
    dot_general x12, matrix products, dot_tn(): lax.dot_general(left, right, (((0,), (0,)), ((), ())), precision=exact, p...  24.6 us
    ppermute x12, starting transfers between devices, spread_async(): lax.ppermute(block, axis, route)  22.2 us
    dot_general x12, matrix products, dot(): lax.dot_general(left, right, (((1,), (0,)), ((), ())), precision=exact, p...  18.8 us
    ppermute x12, waiting for transfers between devices, spread_async(): lax.ppermute(block, axis, route)  18.1 us
  transfers between devices with their start and end apart: 54, of which 18 were waited for; matrix products, arithmetic and copies ran while one was open for 28% of the time, Pallas kernels for 0%

profile of v1, /device:TPU:0, one launch (start us, length us, event | category | flops | bytes accessed | tf_op | source)
XLA Modules:
  0.0 488.3 jit_solution(13128888228008929577)
XLA Ops:
  14.7 4.6 all-to-all-start.1
  29.1 10.4 %all-to-all-done.1 = bf16[4,2,192]{2,1,0:T(2,128)(2,1)S(1)} async-done(((bf16[4,2,192]{2,1,0:T(2,128)(2,1)}), bf16[4,2,192]{2,1,0:T(2,128)(2,1)S(1)}, u32[]{:S(2)}, u32[]{:S(2)}) %all-to-all-start.1) | async-done | bytes 3104 | tf_op jit(solution)/shard_map/all_to_all | solution.py:27
  52.5 5.3 %all-to-all-done.6 = bf16[4,64,256]{2,1,0:T(8,128)(2,1)S(1)} async-done(((bf16[4,64,256]{2,1,0:T(8,128)(2,1)}), bf16[4,64,256]{2,1,0:T(8,128)(2,1)S(1)}, u32[]{:S(2)}, u32[]{:S(2)}) %all-to-all-start.6) | async-done | bytes 131104 | tf_op jit(solution)/shard_map/all_to_all | solution.py:27
  69.1 5.2 %all-to-all-done.3 = bf16[4,64,896]{2,1,0:T(8,128)(2,1)S(1)} async-done(((bf16[4,64,896]{2,1,0:T(8,128)(2,1)}), bf16[4,64,896]{2,1,0:T(8,128)(2,1)S(1)}, u32[]{:S(2)}, u32[]{:S(2)}) %all-to-all-start.3) | async-done | bytes 458784 | tf_op jit(solution)/shard_map/all_to_all | solution.py:27
  75.1 4.1 all-to-all-start
  87.2 4.2 all-to-all-done
  92.7 4.2 all-to-all-start.4
  104.4 20.2 %all-to-all-done.4 = bf16[4,256,896]{2,1,0:T(8,128)(2,1)S(1)} async-done(((bf16[4,256,896]{2,1,0:T(8,128)(2,1)}), bf16[4,256,896]{2,1,0:T(8,128)(2,1)S(1)}, u32[]{:S(2)}, u32[]{:S(2)}) %all-to-all-start.4) | async-done | bytes 1835040 | tf_op jit(solution)/shard_map/all_to_all | solution.py:27
  126.0 7.5 %all-to-all-start.7 = ((bf16[4,256,256]{2,1,0:T(8,128)(2,1)}), bf16[4,256,256]{2,1,0:T(8,128)(2,1)S(1)}, u32[]{:S(2)}, u32[]{:S(2)}) async-start(bf16[4,256,256]{2,1,0:T(8,128)(2,1)} %broadcast_in_dim.268), calls=%async_computation.7 | async-start | bytes 1048576 | tf_op jit(solution)/shard_map/all_to_all | solution.py:27
  184.3 4.5 all-to-all-start.8
  193.0 18.1 %collective-permute-done.8 = bf16[256,2048]{1,0:T(8,128)(2,1)} collective-permute-done((bf16[256,2048]{1,0:T(8,128)(2,1)S(1)}, bf16[256,2048]{1,0:T(8,128)(2,1)}, u32[]{:S(2)}, u32[]{:S(2)}) %collective-permute-start.8) | collective-permute-done | bytes 1048608 | tf_op jit(solution)/shard_map/ppermute | solution.py:47
  242.0 4.4 convolution_convert_fusion
  248.3 4.3 all-to-all-start.9
  256.0 11.1 %all-to-all-done.9 = bf16[4,64,1024]{2,1,0:T(8,128)(2,1)S(1)} async-done(((bf16[4,64,1024]{2,1,0:T(8,128)(2,1)}), bf16[4,64,1024]{2,1,0:T(8,128)(2,1)S(1)}, u32[]{:S(2)}, u32[]{:S(2)}) %all-to-all-start.9) | async-done | bytes 524320 | tf_op jit(solution)/shard_map/all_to_all | solution.py:27
  328.0 7.0 %all-to-all-start.14 = ((f32[4,4,384]{2,1,0:T(4,128)}), f32[4,4,384]{2,1,0:T(4,128)S(1)}, u32[]{:S(2)}, u32[]{:S(2)}) async-start(f32[4,4,384]{2,1,0:T(4,128)} %reshape.487), calls=%async_computation.14 | async-start | bytes 49152 | tf_op jit(solution)/shard_map/all_to_all | solution.py:27
  355.4 4.7 all-to-all-done.15
  363.8 4.0 convolution_convert_fusion.1
  372.3 7.7 %all-to-all-done.16 = bf16[4,256,256]{1,2,0:T(8,128)(2,1)S(1)} async-done(((bf16[4,256,256]{1,2,0:T(8,128)(2,1)}), bf16[4,256,256]{1,2,0:T(8,128)(2,1)S(1)}, u32[]{:S(2)}, u32[]{:S(2)}) %all-to-all-start.16) | async-done | bytes 524320 | tf_op jit(solution)/shard_map/all_to_all | solution.py:27
  390.9 5.0 %all-to-all-start.11 = ((bf16[4,64,1024]{2,1,0:T(8,128)(2,1)}), bf16[4,64,1024]{2,1,0:T(8,128)(2,1)S(1)}, u32[]{:S(2)}, u32[]{:S(2)}) async-start(bf16[4,64,1024]{2,1,0:T(8,128)(2,1)} %fusion.21), calls=%async_computation.11 | async-start | bytes 1048576 | tf_op jit(solution)/shard_map/all_to_all | solution.py:27
  400.8 5.2 %collective-permute-done.35 = bf16[64,1024]{1,0:T(8,128)(2,1)S(1)} collective-permute-done((bf16[64,1024]{1,0:T(8,128)(2,1)S(1)}, bf16[64,1024]{1,0:T(8,128)(2,1)S(1)}, u32[]{:S(2)}, u32[]{:S(2)}) %collective-permute-start.35) | collective-permute-done | bytes 131104 | tf_op jit(solution)/shard_map/ppermute | solution.py:55
  406.0 12.0 %collective-permute-start.33 = (bf16[64,1024]{1,0:T(8,128)(2,1)S(1)}, bf16[64,1024]{1,0:T(8,128)(2,1)S(1)}, u32[]{:S(2)}, u32[]{:S(2)}) collective-permute-start(bf16[64,1024]{1,0:T(8,128)(2,1)S(1)} %get-tuple-element.97), channel_id=1, source_target_pairs={{0,2},{2,4},{4,6},{6,0},{1,3},{3,5},{5,7},{7,1},{8,10},{10,12},{12... | collective-permute-start | bytes 393224 | tf_op jit(solution)/shard_map/ppermute | solution.py:55
  425.8 17.1 %collective-permute-done.25 = bf16[256,2048]{1,0:T(8,128)(2,1)} collective-permute-done((bf16[256,2048]{1,0:T(8,128)(2,1)}, bf16[256,2048]{1,0:T(8,128)(2,1)}, u32[]{:S(2)}, u32[]{:S(2)}) %collective-permute-start.25) | collective-permute-done | bytes 1048608 | tf_op jit(solution)/shard_map/ppermute | solution.py:55
  453.9 4.1 all-to-all-start.13
  458.0 18.9 %collective-permute-done.28 = bf16[64,2048]{1,0:T(8,128)(2,1)} collective-permute-done((bf16[64,2048]{1,0:T(8,128)(2,1)}, bf16[64,2048]{1,0:T(8,128)(2,1)}, u32[]{:S(2)}, u32[]{:S(2)}) %collective-permute-start.28) | collective-permute-done | bytes 262176 | tf_op jit(solution)/shard_map/ppermute | solution.py:55
  (618 shorter events, 291.4 us)
Async XLA Ops:
  2.5 94.5 %collective-permute-start.4 = (bf16[64,2048]{1,0:T(8,128)(2,1)}, bf16[64,2048]{1,0:T(8,128)(2,1)}, u32[]{:S(2)}, u32[]{:S(2)}) collective-permute-start(bf16[64,2048]{1,0:T(8,128)(2,1)} %bitcast.167), channel_id=1, source_target_pairs={{0,2},{2,4},{4,6},{6,0},{1,3},{3,5},{5,7},{7,1},{8,10},{10,12},{12... | collective-permute-start | bytes 786440 | tf_op jit(solution)/shard_map/ppermute | solution.py:47
  5.5 92.4 %collective-permute-start.5 = (bf16[64,2048]{1,0:T(8,128)(2,1)}, bf16[64,2048]{1,0:T(8,128)(2,1)}, u32[]{:S(2)}, u32[]{:S(2)}) collective-permute-start(bf16[64,2048]{1,0:T(8,128)(2,1)} %bitcast.167), channel_id=1, source_target_pairs={{0,4},{2,6},{4,0},{6,2},{1,5},{3,7},{5,1},{7,3},{8,12},{10,14},{12... | collective-permute-start | bytes 786440 | tf_op jit(solution)/shard_map/ppermute | solution.py:47
  8.1 152.6 %collective-permute-start.6 = (bf16[64,2048]{1,0:T(8,128)(2,1)}, bf16[64,2048]{1,0:T(8,128)(2,1)}, u32[]{:S(2)}, u32[]{:S(2)}) collective-permute-start(bf16[64,2048]{1,0:T(8,128)(2,1)} %bitcast.167), channel_id=1, source_target_pairs={{0,6},{2,0},{4,2},{6,4},{1,7},{3,1},{5,3},{7,5},{8,14},{10,8},{12,... | collective-permute-start | bytes 786440 | tf_op jit(solution)/shard_map/ppermute | solution.py:47
  9.5 55.8 %collective-permute-start.10 = (bf16[64,1024]{1,0:T(8,128)(2,1)}, bf16[64,1024]{1,0:T(8,128)(2,1)S(1)}, u32[]{:S(2)}, u32[]{:S(2)}) collective-permute-start(bf16[64,1024]{1,0:T(8,128)(2,1)} %bitcast.371), channel_id=1, source_target_pairs={{0,2},{2,4},{4,6},{6,0},{1,3},{3,5},{5,7},{7,1},{8,10},{10,12},{12... | collective-permute-start | bytes 393224 | tf_op jit(solution)/shard_map/ppermute | solution.py:47
  10.1 69.8 %collective-permute-start.11 = (bf16[64,1024]{1,0:T(8,128)(2,1)}, bf16[64,1024]{1,0:T(8,128)(2,1)S(1)}, u32[]{:S(2)}, u32[]{:S(2)}) collective-permute-start(bf16[64,1024]{1,0:T(8,128)(2,1)} %bitcast.372), channel_id=1, source_target_pairs={{0,4},{2,6},{4,0},{6,2},{1,5},{3,7},{5,1},{7,3},{8,12},{10,14},{12... | collective-permute-start | bytes 393224 | tf_op jit(solution)/shard_map/ppermute | solution.py:47
  81.3 87.0 %collective-permute-start.13 = (bf16[256,1024]{1,0:T(8,128)(2,1)}, bf16[256,1024]{1,0:T(8,128)(2,1)}, u32[]{:S(2)}, u32[]{:S(2)}) collective-permute-start(bf16[256,1024]{1,0:T(8,128)(2,1)} %bitcast.65), channel_id=1, source_target_pairs={{0,8},{8,16},{16,24},{24,0},{1,9},{9,17},{17,25},{25,1},{2,10},{10... | collective-permute-start | bytes 1572872 | tf_op jit(solution)/shard_map/ppermute | solution.py:47
  82.3 89.4 %collective-permute-start.14 = (bf16[256,1024]{1,0:T(8,128)(2,1)}, bf16[256,1024]{1,0:T(8,128)(2,1)}, u32[]{:S(2)}, u32[]{:S(2)}) collective-permute-start(bf16[256,1024]{1,0:T(8,128)(2,1)} %bitcast.65), channel_id=1, source_target_pairs={{0,16},{8,24},{16,0},{24,8},{1,17},{9,25},{17,1},{25,9},{2,18},{10... | collective-permute-start | bytes 1572872 | tf_op jit(solution)/shard_map/ppermute | solution.py:47
  92.7 31.8 %all-to-all-start.4 = ((bf16[4,256,896]{2,1,0:T(8,128)(2,1)}), bf16[4,256,896]{2,1,0:T(8,128)(2,1)S(1)}, u32[]{:S(2)}, u32[]{:S(2)}) async-start(bf16[4,256,896]{2,1,0:T(8,128)(2,1)} %broadcast_in_dim.258), calls=%async_computation.4 | async-start | bytes 3670016 | tf_op jit(solution)/shard_map/all_to_all | solution.py:27
  98.0 90.8 %collective-permute-start.15 = (bf16[256,1024]{1,0:T(8,128)(2,1)}, bf16[256,1024]{1,0:T(8,128)(2,1)}, u32[]{:S(2)}, u32[]{:S(2)}) collective-permute-start(bf16[256,1024]{1,0:T(8,128)(2,1)} %bitcast.65), channel_id=1, source_target_pairs={{0,24},{8,0},{16,8},{24,16},{1,25},{9,1},{17,9},{25,17},{2,26},{10... | collective-permute-start | bytes 1572872 | tf_op jit(solution)/shard_map/ppermute | solution.py:47
  162.6 28.1 %collective-permute-start.7 = (bf16[256,2048]{1,0:T(8,128)(2,1)S(1)}, bf16[256,2048]{1,0:T(8,128)(2,1)}, u32[]{:S(2)}, u32[]{:S(2)}) collective-permute-start(bf16[256,2048]{1,0:T(8,128)(2,1)S(1)} %bitcast.334), channel_id=1, source_target_pairs={{0,8},{8,16},{16,24},{24,0},{1,9},{9,17},{17,25},{25,1},{2,10},{10... | collective-permute-start | bytes 3145736 | tf_op jit(solution)/shard_map/ppermute | solution.py:47
  168.2 42.8 %collective-permute-start.8 = (bf16[256,2048]{1,0:T(8,128)(2,1)S(1)}, bf16[256,2048]{1,0:T(8,128)(2,1)}, u32[]{:S(2)}, u32[]{:S(2)}) collective-permute-start(bf16[256,2048]{1,0:T(8,128)(2,1)S(1)} %bitcast.336), channel_id=1, source_target_pairs={{0,16},{8,24},{16,0},{24,8},{1,17},{9,25},{17,1},{25,9},{2,18},{10... | collective-permute-start | bytes 3145736 | tf_op jit(solution)/shard_map/ppermute | solution.py:47
  173.5 44.7 %collective-permute-start.9 = (bf16[256,2048]{1,0:T(8,128)(2,1)S(1)}, bf16[256,2048]{1,0:T(8,128)(2,1)}, u32[]{:S(2)}, u32[]{:S(2)}) collective-permute-start(bf16[256,2048]{1,0:T(8,128)(2,1)S(1)} %bitcast.337), channel_id=1, source_target_pairs={{0,24},{8,0},{16,8},{24,16},{1,25},{9,1},{17,9},{25,17},{2,26},{10... | collective-permute-start | bytes 3145736 | tf_op jit(solution)/shard_map/ppermute | solution.py:47
  184.3 30.3 %all-to-all-start.8 = ((bf16[4,64,2048]{2,1,0:T(8,128)(2,1)}), bf16[4,64,2048]{2,1,0:T(8,128)(2,1)}, u32[]{:S(2)}, u32[]{:S(2)}) async-start(bf16[4,64,2048]{2,1,0:T(8,128)(2,1)} %fusion.3), calls=%async_computation.8 | async-start | bytes 2097152 | tf_op jit(solution)/shard_map/all_to_all | solution.py:27
  324.2 64.6 %collective-permute-start.21 = (bf16[4,64,1024]{2,1,0:T(8,128)(2,1)}, bf16[4,64,1024]{2,1,0:T(8,128)(2,1)}, u32[]{:S(2)}, u32[]{:S(2)}) collective-permute-start(bf16[4,64,1024]{2,1,0:T(8,128)(2,1)} %fusion.43), channel_id=1, source_target_pairs={{0,1},{1,0},{2,3},{3,2},{4,5},{5,4},{6,7},{7,6},{8,9},{9,8},{10,11... | collective-permute-start | bytes 1572872 | tf_op jit(solution)/shard_map/ppermute | solution.py:17
  346.6 37.6 %collective-permute-start.32 = (bf16[256,1024]{1,0:T(8,128)(2,1)}, bf16[256,1024]{1,0:T(8,128)(2,1)}, u32[]{:S(2)}, u32[]{:S(2)}) collective-permute-start(bf16[256,1024]{1,0:T(8,128)(2,1)} %get-tuple-element.71), channel_id=1, source_target_pairs={{0,24},{8,0},{16,8},{24,16},{1,25},{9,1},{17,9},{25,17},{2,26},{10... | collective-permute-start | bytes 1572872 | tf_op jit(solution)/shard_map/ppermute | solution.py:55
  349.6 35.8 %collective-permute-start.31 = (bf16[256,1024]{1,0:T(8,128)(2,1)}, bf16[256,1024]{1,0:T(8,128)(2,1)}, u32[]{:S(2)}, u32[]{:S(2)}) collective-permute-start(bf16[256,1024]{1,0:T(8,128)(2,1)} %get-tuple-element.72), channel_id=1, source_target_pairs={{0,16},{8,24},{16,0},{24,8},{1,17},{9,25},{17,1},{25,9},{2,18},{10... | collective-permute-start | bytes 1572872 | tf_op jit(solution)/shard_map/ppermute | solution.py:55
  350.1 37.0 %collective-permute-start.30 = (bf16[256,1024]{1,0:T(8,128)(2,1)}, bf16[256,1024]{1,0:T(8,128)(2,1)}, u32[]{:S(2)}, u32[]{:S(2)}) collective-permute-start(bf16[256,1024]{1,0:T(8,128)(2,1)} %get-tuple-element.70), channel_id=1, source_target_pairs={{0,8},{8,16},{16,24},{24,0},{1,9},{9,17},{17,25},{25,1},{2,10},{10... | collective-permute-start | bytes 1572872 | tf_op jit(solution)/shard_map/ppermute | solution.py:55
  367.8 58.0 %collective-permute-start.26 = (bf16[256,2048]{1,0:T(8,128)(2,1)}, bf16[256,2048]{1,0:T(8,128)(2,1)}, u32[]{:S(2)}, u32[]{:S(2)}) collective-permute-start(bf16[256,2048]{1,0:T(8,128)(2,1)} %get-tuple-element.67), channel_id=1, source_target_pairs={{0,24},{8,0},{16,8},{24,16},{1,25},{9,1},{17,9},{25,17},{2,26},{10... | collective-permute-start | bytes 3145736 | tf_op jit(solution)/shard_map/ppermute | solution.py:55
  384.2 58.7 %collective-permute-start.25 = (bf16[256,2048]{1,0:T(8,128)(2,1)}, bf16[256,2048]{1,0:T(8,128)(2,1)}, u32[]{:S(2)}, u32[]{:S(2)}) collective-permute-start(bf16[256,2048]{1,0:T(8,128)(2,1)} %get-tuple-element.68), channel_id=1, source_target_pairs={{0,16},{8,24},{16,0},{24,8},{1,17},{9,25},{17,1},{25,9},{2,18},{10... | collective-permute-start | bytes 3145736 | tf_op jit(solution)/shard_map/ppermute | solution.py:55
  385.3 57.6 %collective-permute-start.24 = (bf16[256,2048]{1,0:T(8,128)(2,1)}, bf16[256,2048]{1,0:T(8,128)(2,1)}, u32[]{:S(2)}, u32[]{:S(2)}) collective-permute-start(bf16[256,2048]{1,0:T(8,128)(2,1)} %get-tuple-element.66), channel_id=1, source_target_pairs={{0,8},{8,16},{16,24},{24,0},{1,9},{9,17},{17,25},{25,1},{2,10},{10... | collective-permute-start | bytes 3145736 | tf_op jit(solution)/shard_map/ppermute | solution.py:55
  390.9 30.4 %all-to-all-start.11 = ((bf16[4,64,1024]{2,1,0:T(8,128)(2,1)}), bf16[4,64,1024]{2,1,0:T(8,128)(2,1)S(1)}, u32[]{:S(2)}, u32[]{:S(2)}) async-start(bf16[4,64,1024]{2,1,0:T(8,128)(2,1)} %fusion.21), calls=%async_computation.11 | async-start | bytes 1048576 | tf_op jit(solution)/shard_map/all_to_all | solution.py:27
  422.1 30.6 %all-to-all-start.12 = ((bf16[4,256,896]{2,1,0:T(8,128)(2,1)}), bf16[4,256,896]{2,1,0:T(8,128)(2,1)S(1)}, u32[]{:S(2)}, u32[]{:S(2)}) async-start(bf16[4,256,896]{2,1,0:T(8,128)(2,1)} %bitcast.348), calls=%async_computation.12 | async-start | bytes 3670016 | tf_op jit(solution)/shard_map/all_to_all | solution.py:27
  452.7 26.7 %collective-permute-start.22 = (f32[64,1024]{1,0:T(8,128)}, f32[64,1024]{1,0:T(8,128)S(1)}, u32[]{:S(2)}, u32[]{:S(2)}) collective-permute-start(f32[64,1024]{1,0:T(8,128)} %fusion.57), channel_id=1, source_target_pairs={{0,1},{1,0},{2,3},{3,2},{4,5},{5,4},{6,7},{7,6},{8,9},{9,8},{10,11... | collective-permute-start | bytes 786440 | tf_op jit(solution)/shard_map/ppermute | solution.py:17
  453.9 27.4 %all-to-all-start.13 = ((bf16[4,64,896]{2,1,0:T(8,128)(2,1)}), bf16[4,64,896]{2,1,0:T(8,128)(2,1)S(1)}, u32[]{:S(2)}, u32[]{:S(2)}) async-start(bf16[4,64,896]{2,1,0:T(8,128)(2,1)} %bitcast.105), calls=%async_computation.13 | async-start | bytes 917504 | tf_op jit(solution)/shard_map/all_to_all | solution.py:27
  (162 other events, 1310.7 us)
